TPU v7x, 32 devices: a whole 2x2x4 slice. The times are simulated.
32 devices in a mesh: groups: 2 (over x), expert: 16 (over z, y, core).
Axes of the slice: x: 2, y: 2, z: 4, core: 2. Of those that a mesh axis runs over, the one named last changes fastest.
Arguments:
- tokens_in: bfloat16 [4096, 1024], P(('groups', 'expert')), parts along dimension 0, may hold values from -6 to 6
- grad_out: bfloat16 [4096, 1024], P(('groups', 'expert')), parts along dimension 0, may hold values from -6 to 6
- gates: bfloat16 [4096, 8], P(('groups', 'expert')), parts along dimension 0, may hold values from 0.049804688 to 0.5
- expert_ids: int32 [4096, 8], P(('groups', 'expert')), parts along dimension 0, may hold values from 0 to 15, as said below
- replica_table: int32 [32], P('groups'), parts along dimension 0, may hold values from 0 to 15, as said below
- w_gate: bfloat16 [16, 1024, 384], P('expert'), may hold values from -0.1875 to 0.1875
- w_up: bfloat16 [16, 1024, 384], P('expert'), may hold values from -0.1875 to 0.1875
- w_down: bfloat16 [16, 384, 1024], P('expert'), may hold values from -0.3125 to 0.3125
Outputs:
- grad_tokens: bfloat16 [4096, 1024], P(('groups', 'expert')), parts along dimension 0
- grad_gates: bfloat16 [4096, 8], P(('groups', 'expert')), parts along dimension 0
- grad_w_gate: bfloat16 [32, 1024, 384], P(('groups', 'expert')), parts along dimension 0
- grad_w_up: bfloat16 [32, 1024, 384], P(('groups', 'expert')), parts along dimension 0
- grad_w_down: bfloat16 [32, 384, 1024], P(('groups', 'expert')), parts along dimension 0
There are 2 independent parts, one for each index of `groups`. A program takes and returns all parts, laid end to end along the dimension named above; an argument that names none is the same for every part. Nothing has to cross between parts.
Inputs may be any that keep to these rules, and one draw needn't show every extreme that they name: `expert_ids`: each row names 8 different experts. `replica_table`: entry d is the expert whose weights device d holds in its replica slot.
All inputs are finite; a program needn't handle non-finite values.
Results may differ from a plain program's by a relative error of at most 0.0057.
Values may be sent and summed in bfloat16 or wider, within the bound.
A program may use at most 128 MiB of HBM per device.

v0:
```python
import jax
import jax.numpy as jnp
from jax import lax
from jax.experimental import pallas as pl
from jax.experimental.pallas import tpu as pltpu
from jax.sharding import PartitionSpec as P

TOP = 8
ROWS_PER_CHUNK = 4096

contract_rows = (((0,), (0,)), ((), ()))
contract_cols = (((1,), (1,)), ((), ()))

MESH = pl.DeviceIdType.MESH
VMEM_GRANT = 48 * 2**20


def place(depth):
    me = lax.axis_index("expert")
    z, y, c = me // 4, (me // 2) % 2, me % 2
    return me, z, y, c, depth - 1


def index_of(z, y, c):
    return (z * 2 + y) * 2 + c


def greet(z, y, c, last):
    sem = pltpu.get_barrier_semaphore()

    def hello(peer):
        pl.semaphore_signal(sem, inc=1, device_id={"expert": peer}, device_id_type=MESH)

    hello(index_of(z, y, 1 - c))
    hello(index_of(z, 1 - y, c))
    pl.when(z > 0)(lambda: hello(index_of(z - 1, y, c)))
    pl.when(z < last)(lambda: hello(index_of(z + 1, y, c)))
    pl.semaphore_wait(sem, 2 + (z > 0).astype(jnp.int32) + (z < last).astype(jnp.int32))


class Sender:
    def __init__(self, sems):
        self.sems, self.used, self.pending = sems, 0, []

    def send(self, cond, make):
        slot = self.used
        self.used += 1
        if cond is None:
            make(self.sems.at[slot]).start()
        else:
            pl.when(cond)(lambda: make(self.sems.at[slot]).start())
        self.pending.append((cond, make, slot))

    def drain(self):
        for cond, make, slot in self.pending:
            if cond is None:
                make(self.sems.at[slot]).wait_send()
            else:
                pl.when(cond)(lambda make=make, slot=slot: make(self.sems.at[slot]).wait_send())


def remote(src, dst, recv_sem, peer):
    return lambda send_sem: pltpu.make_async_remote_copy(
        src_ref=src(), dst_ref=dst(), send_sem=send_sem, recv_sem=recv_sem(),
        device_id={"expert": peer()}, device_id_type=MESH,
    )


def both(p, q):
    return q if p is None else p & q


def gather_kernel(
    depth, split, x_ref, wg_ref, wu_ref, wd_ref, buf, da_ref, db_ref, hg_ref, dx_ref, gg_ref,
    send_sems, recv_sems, local_sem,
):
    me, z, y, c, last = place(depth)
    tok = x_ref.shape[0]
    rows = (pl.ds(0, split), pl.ds(split, tok - split))
    local = pltpu.make_async_copy(x_ref, buf.at[me], local_sem)
    local.start()
    greet(z, y, c, last)
    out = Sender(send_sems)

    def push(cond, b, part, peer, own=False):
        src = (lambda: x_ref.at[rows[part]]) if own else (lambda: buf.at[b(), rows[part]])
        out.send(
            cond,
            remote(src, lambda: buf.at[b(), rows[part]], lambda: recv_sems.at[b(), part], peer),
        )

    def arrived(b, part):
        pltpu.make_async_copy(
            buf.at[b, rows[part]], buf.at[b, rows[part]], recv_sems.at[b, part]
        ).wait()

    up = lambda: index_of(z + 1, y, c)
    down = lambda: index_of(z - 1, y, c)
    over = lambda: index_of(z, 1 - y, c)
    twin = lambda: index_of(z, y, 1 - c)
    can_up, can_down = z < last, z > 0
    mine = lambda: me
    push(None, mine, 0, over, True)
    push(can_up, mine, 1, up, True)
    push(can_down, mine, 1, down, True)
    push(can_up, mine, 0, up, True)
    push(can_down, mine, 0, down, True)
    push(None, mine, 1, over, True)
    push(None, mine, 0, twin, True)
    push(None, mine, 1, twin, True)
    across = lambda: index_of(z, 1 - y, c)
    arrived(across(), 0)
    push(can_up, across, 0, up)
    push(can_down, across, 0, down)
    push(None, across, 0, twin)

    def sides_at(d):
        return ((None, 0),) if d == 0 else ((z >= d, -d), (z + d <= last, d))

    width = dx_ref.shape[2]
    f32 = jnp.float32
    bf16 = jnp.bfloat16

    def level(zz):
        for part in range(2):
            for yy in range(2):
                arrived(index_of(zz, yy, 1 - c), part)

        def pair(i, carry):
            at = pl.ds(zz * 4 + 2 * i, 2)
            x = buf[at, :, pl.ds(0, width)].reshape(2 * tok, width)
            dy = buf[at, :, pl.ds(width, width)].reshape(2 * tok, width)
            gates = buf[at, :, pl.ds(2 * width, buf.shape[2] - 2 * width)].reshape(2 * tok, -1)
            mine = lax.broadcasted_iota(jnp.int32, gates.shape, 1) == me
            gate = jnp.sum(jnp.where(mine, gates.astype(f32), 0.0), axis=1, keepdims=True)
            gate_grad, hg, da, db, dx = row_grads(
                x, dy, gate, wg_ref[...], wu_ref[...], wd_ref[...]
            )
            hg_ref[at] = hg.reshape(2, tok, -1)
            da_ref[at] = da.reshape(2, tok, -1)
            db_ref[at] = db.reshape(2, tok, -1)
            dx_ref[at] = dx.astype(bf16).reshape(2, tok, width)
            gg_ref[at] = jnp.where(mine, gate_grad, 0.0).astype(bf16).reshape(2, tok, -1)
            return carry

        lax.fori_loop(0, 2, pair, 0)

    def levels(d):
        for cond, off in sides_at(d):
            if cond is None:
                level(z)
            else:
                pl.when(cond)(lambda: level(z + off))

    def crossed(d):
        sides = sides_at(d)
        for cond, off in sides:
            b = lambda off=off: index_of(z + off, 1 - y, c)
            if cond is None:
                arrived(b(), 1)
            else:
                pl.when(cond)(lambda: arrived(b(), 1))
            push(cond, b, 1, twin)

    for d in range(1, depth):
        own = [
            (z >= d, lambda d=d: index_of(z - d, y, c), can_up, up),
            (z + d <= last, lambda d=d: index_of(z + d, y, c), can_down, down),
        ]
        far = [
            (z >= d, lambda d=d: index_of(z - d, 1 - y, c), can_up, up),
            (z + d <= last, lambda d=d: index_of(z + d, 1 - y, c), can_down, down),
        ]
        for part, group in ((1, own), (0, own), (0, far)):
            for here, b, more, onward in group:
                pl.when(here)(lambda: arrived(b(), part))
                push(both(here, more), b, part, onward)
                if part == 1:
                    push(here, b, 1, over)
                push(here, b, part, twin)
        crossed(d - 1)
        if d == 1:
            local.wait()
        levels(d - 1)
    crossed(depth - 1)
    if depth == 1:
        local.wait()
    levels(depth - 1)
    out.drain()


def gather_rows(x, gate_w, up_w, down_w, devices, split):
    depth = devices // 4
    tok, wide = x.shape
    hidden, width = down_w.shape
    sizes = (wide, hidden, hidden, hidden, width, wide - 2 * width)
    return pl.pallas_call(
        lambda *refs: gather_kernel(depth, split, *refs),
        out_shape=[jax.ShapeDtypeStruct((devices, tok, n), x.dtype) for n in sizes],
        in_specs=[pl.BlockSpec(memory_space=pltpu.VMEM)] * 4,
        out_specs=[pl.BlockSpec(memory_space=pltpu.VMEM)] * 6,
        scratch_shapes=[
            pltpu.SemaphoreType.DMA((16 * depth,)),
            pltpu.SemaphoreType.DMA((devices, 2)),
            pltpu.SemaphoreType.DMA,
        ],
        compiler_params=pltpu.CompilerParams(
            collective_id=0, has_side_effects=True, vmem_limit_bytes=VMEM_GRANT
        ),
    )(x, gate_w, up_w, down_w)


def scatter_kernel(
    depth, split, part_ref, gate_ref, out_ref, rc, acc0, acc1, accx, ry1, rz0, rz1, ry0,
    send_sems, rc_sems, ry1_sems, rz0_sems, rz1_sems, ry0_sem,
):
    me, z, y, c, last = place(depth)
    tok, wide = out_ref.shape
    main = part_ref.shape[2]
    spans = ((part_ref, pl.ds(0, main)), (gate_ref, pl.ds(main, wide - main)))
    head, tail = pl.ds(0, split), pl.ds(split, tok - split)
    greet(z, y, c, last)
    out = Sender(send_sems)
    f32 = jnp.float32
    bf16 = jnp.bfloat16
    up = lambda: index_of(z + 1, y, c)
    down = lambda: index_of(z - 1, y, c)
    over = lambda: index_of(z, 1 - y, c)
    twin = lambda: index_of(z, y, 1 - c)

    def landed(ref, sem):
        pltpu.make_async_copy(ref, ref, sem).wait()

    order = []
    for k in range(depth // 2):
        order += [depth - 1 - k, k]
    if depth % 2:
        order.append(depth // 2)
    for zz in order:
        for off in (1, 0):
            yy = (y + off) % 2
            for k, (src, span) in enumerate(spans):
                out.send(
                    None,
                    remote(
                        lambda zz=zz, yy=yy, src=src: src.at[index_of(zz, yy, 1 - c)],
                        lambda zz=zz, yy=yy, span=span: rc.at[zz, yy, :, span],
                        lambda zz=zz, yy=yy, k=k: rc_sems.at[zz, yy, k],
                        twin,
                    ),
                )
    for zz in order:
        for off in (1, 0):
            yy = (y + off) % 2
            b = index_of(zz, yy, c)
            rest = accx if off else acc1
            for k, (src, span) in enumerate(spans):
                landed(rc.at[zz, yy, :, span], rc_sems.at[zz, yy, k])
                acc0[zz, yy, :, span] = (
                    src[b, head].astype(f32) + rc[zz, yy, head, span].astype(f32)
                ).astype(bf16)
                rest[zz, :, span] = (
                    src[b, tail].astype(f32) + rc[zz, yy, tail, span].astype(f32)
                ).astype(bf16)
            if off:
                out.send(
                    None,
                    remote(
                        lambda zz=zz: accx.at[zz], lambda zz=zz: ry1.at[zz],
                        lambda zz=zz: ry1_sems.at[zz], over,
                    ),
                )

    def add_chain(way, zz):
        landed(rz1.at[way, zz], rz1_sems.at[way, zz])
        acc1[zz] = (acc1[zz].astype(f32) + rz1[way, zz].astype(f32)).astype(bf16)
        landed(rz0.at[way, zz], rz0_sems.at[way, zz])
        acc0[zz] = (acc0[zz].astype(f32) + rz0[way, zz].astype(f32)).astype(bf16)

    for zz in order:
        landed(ry1.at[zz], ry1_sems.at[zz])
        acc1[zz] = (acc1[zz].astype(f32) + ry1[zz].astype(f32)).astype(bf16)
        for way, going, has, peer in ((0, z < zz, z > 0, up), (1, z > zz, z < last, down)):
            pl.when(both(going, has))(lambda: add_chain(way, zz))
            out.send(
                going,
                remote(
                    lambda zz=zz: acc1.at[zz], lambda way=way, zz=zz: rz1.at[way, zz],
                    lambda way=way, zz=zz: rz1_sems.at[way, zz], peer,
                ),
            )
            out.send(
                going,
                remote(
                    lambda zz=zz: acc0.at[zz], lambda way=way, zz=zz: rz0.at[way, zz],
                    lambda way=way, zz=zz: rz0_sems.at[way, zz], peer,
                ),
            )
    pl.when(z > 0)(lambda: add_chain(0, z))
    pl.when(z < last)(lambda: add_chain(1, z))
    out.send(
        None,
        remote(lambda: acc0.at[z, 1 - y], lambda: ry0, lambda: ry0_sem, over),
    )
    out_ref[tail] = acc1[z]
    landed(ry0, ry0_sem)
    out_ref[head] = (acc0[z, y].astype(f32) + ry0[...].astype(f32)).astype(bf16)
    out.drain()


def scatter_rows(part, gate, devices, split):
    depth = devices // 4
    tok, wide = part.shape[1], part.shape[2] + gate.shape[2]
    rest = tok - split
    bf = lambda *shape: pltpu.VMEM(shape + (wide,), jnp.bfloat16)
    dma = pltpu.SemaphoreType.DMA
    return pl.pallas_call(
        lambda *refs: scatter_kernel(depth, split, *refs),
        out_shape=jax.ShapeDtypeStruct((tok, wide), part.dtype),
        in_specs=[pl.BlockSpec(memory_space=pltpu.VMEM)] * 2,
        out_specs=pl.BlockSpec(memory_space=pltpu.VMEM),
        scratch_shapes=[
            bf(depth, 2, tok), bf(depth, 2, split), bf(depth, rest), bf(depth, rest),
            bf(depth, rest), bf(2, depth, 2, split), bf(2, depth, rest), bf(split),
            dma((9 * depth + 2,)), dma((depth, 2, 2)), dma((depth,)), dma((2, depth)),
            dma((2, depth)), dma,
        ],
        compiler_params=pltpu.CompilerParams(
            collective_id=1, has_side_effects=True, vmem_limit_bytes=VMEM_GRANT
        ),
    )(part, gate)


def keep_plan(gates, row_ids, replica_table, source, devices, home_cap, rep_cap):
    tok = row_ids.shape[0]
    experts = jnp.arange(devices, dtype=jnp.int32)
    hot = row_ids[:, :, None] == experts[None, None, :]
    named = jnp.any(hot, axis=1)
    dense_gate = jnp.sum(jnp.where(hot, gates.astype(jnp.float32)[:, :, None], 0.0), axis=1)
    copies = 1 + jnp.sum((replica_table[:, None] == experts[None, :]).astype(jnp.int32), axis=0)
    order = jnp.arange(tok, dtype=jnp.int32)
    earlier = (order[:, None] > order[None, :]).astype(jnp.bfloat16)
    rank = jnp.dot(earlier, named.astype(jnp.bfloat16), preferred_element_type=jnp.float32)
    many = copies.astype(jnp.float32)[None, :]
    position = jnp.floor((rank + 0.5) / many)
    turn = rank + source.astype(jnp.float32)
    copy_index = turn - many * jnp.floor((turn + 0.5) / many)
    limit = jnp.where(copy_index < 0.5, float(home_cap), float(rep_cap))
    kept = named & (position < limit)
    return jnp.where(kept, dense_gate, 0.0).astype(jnp.bfloat16)


def row_grads(x, dy, gate, gate_w, up_w, down_w):
    a = jnp.dot(x, gate_w, preferred_element_type=jnp.float32)
    b = jnp.dot(x, up_w, preferred_element_type=jnp.float32)
    u = lax.dot_general(dy, down_w, contract_cols, preferred_element_type=jnp.float32)
    sig = jax.nn.sigmoid(a)
    act = a * sig
    product = act * b
    hidden = product.astype(jnp.bfloat16).astype(jnp.float32)
    gate_grad = jnp.sum(hidden * u, axis=1, keepdims=True)
    gate_grad = jnp.where(gate > 0, gate_grad, 0.0)
    hg = (gate * product).astype(jnp.bfloat16)
    gu = gate * u
    da = (gu * b * sig * (1.0 + a * (1.0 - sig))).astype(jnp.bfloat16)
    db = (gu * act).astype(jnp.bfloat16)
    dx = lax.dot_general(da, gate_w, contract_cols, preferred_element_type=jnp.float32)
    dx = dx + lax.dot_general(db, up_w, contract_cols, preferred_element_type=jnp.float32)
    return gate_grad, hg, da, db, dx


def weight_grads(x, dy, hg, da, db):
    dwg = lax.dot_general(x, da, contract_rows, preferred_element_type=jnp.float32)
    dwu = lax.dot_general(x, db, contract_rows, preferred_element_type=jnp.float32)
    dwd = lax.dot_general(hg, dy, contract_rows, preferred_element_type=jnp.float32)
    return dwg, dwu, dwd


def on_device(tokens_in, grad_out, gates, expert_ids, replica_table, w_gate, w_up, w_down):
    devices = lax.axis_size("expert")
    me = lax.axis_index("expert")
    tok, width = tokens_in.shape
    home_cap = max(2, 5 * tok * TOP // (4 * devices))
    rep_cap = max(2, tok * TOP // (2 * devices))
    kept_gate = keep_plan(gates, expert_ids, replica_table, me, devices, home_cap, rep_cap)
    lanes = -(-devices // 128) * 128
    kept_gate = jnp.pad(kept_gate, ((0, 0), (0, lanes - devices)))
    payload = jnp.concatenate([tokens_in, grad_out, kept_gate], axis=1)
    chunks = max(1, devices * tok // ROWS_PER_CHUNK)
    part = tok // chunks
    relayed = chunks == 1 and devices % 4 == 0 and tok % 32 == 0
    split = max(16, tok // 8 // 16 * 16)
    mine = jnp.arange(lanes, dtype=jnp.int32)[None, :] == me
    backs, sums = [], None
    for c in range(chunks):
        if relayed:
            rows, da, db, hg, dx, spread = gather_rows(
                payload, w_gate[0], w_up[0], w_down[0], devices, split
            )
            backs.append(scatter_rows(dx, spread, devices, split))
            rows, da, db, hg = [v.reshape(devices * tok, -1) for v in (rows, da, db, hg)]
        else:
            rows = lax.all_gather(payload[c * part : (c + 1) * part], "expert", axis=0, tiled=True)
            gate = jnp.sum(
                jnp.where(mine, rows[:, 2 * width :].astype(jnp.float32), 0.0),
                axis=1,
                keepdims=True,
            )
            gate_grad, hg, da, db, dx = row_grads(
                rows[:, :width], rows[:, width : 2 * width], gate, w_gate[0], w_up[0], w_down[0]
            )
            spread = jnp.where(mine, gate_grad, 0.0).astype(jnp.bfloat16)
            back = jnp.concatenate([dx.astype(jnp.bfloat16), spread], axis=1)
            backs.append(lax.psum_scatter(back, "expert", scatter_dimension=0, tiled=True))
        grads = weight_grads(rows[:, :width], rows[:, width : 2 * width], hg, da, db)
        sums = grads if sums is None else [p + q for p, q in zip(sums, grads)]
        if c + 1 < chunks:
            payload, sums = lax.optimization_barrier((payload, sums))
    back = jnp.concatenate(backs, axis=0)
    experts = jnp.arange(devices, dtype=jnp.int32)
    hot = expert_ids[:, :, None] == experts[None, None, :]
    picked = jnp.where(hot, back[:, None, width : width + devices].astype(jnp.float32), 0.0)
    grad_gates = jnp.sum(picked, axis=2).astype(jnp.bfloat16)
    return (back[:, :width], grad_gates, *[g.astype(jnp.bfloat16)[None] for g in sums])


def solution(mesh):
    return jax.shard_map(
        on_device,
        mesh=mesh,
        in_specs=(
            P(("groups", "expert"), None),
            P(("groups", "expert"), None),
            P(("groups", "expert"), None),
            P(("groups", "expert"), None),
            P("groups"),
            P("expert", None, None),
            P("expert", None, None),
            P("expert", None, None),
        ),
        out_specs=(
            P(("groups", "expert"), None),
            P(("groups", "expert"), None),
            P(("groups", "expert"), None, None),
            P(("groups", "expert"), None, None),
            P(("groups", "expert"), None, None),
        ),
        check_vma=False,
    )
```

profile of v0, /device:TPU:10, one launch (start us, length us, event | category | flops | bytes accessed | tf_op | source)
XLA Modules:
  0.0 135.3 jit_solution(9234451378231862616)
XLA Ops:
  0.6 0.0 copy-start.2
  0.6 0.0 copy-start.1
  0.7 0.9 convert_reduce_fusion
  1.5 0.7 fusion.26
  2.2 0.7 convert_element_type.42
  2.9 0.7 select_reduce_fusion.1
  3.6 0.1 copy.27
  3.7 0.1 copy.28
  3.8 0.2 select_convert_fusion
  4.0 1.1 fusion.25.refs_0_
  5.1 0.0 copy-done.2
  5.1 0.0 copy-done.1
  5.1 0.0 copy-start.3
  5.1 1.1 copy-done.3
  6.3 56.8 %shard_map.119 = (bf16[16,128,2176]{2,1,0:T(8,128)(2,1)}, bf16[16,128,384]{2,1,0:T(8,128)(2,1)S(1)}, bf16[16,128,384]{2,1,0:T(8,128)(2,1)}, bf16[16,128,384]{2,1...) custom-call(bf16[128,2176]{1,0:T(8,128)(2,1)S(1)} %fusion.25.refs_0_, ...), custom_call_target="tpu_custom_call" | custom-call | tf_op jit(solution)/shard_map/pallas_call | solution.py:197
  63.1 0.0 copy-start
  63.1 2.2 %copy-done = bf16[16,128,1024]{2,1,0:T(8,128)(2,1)S(1)} copy-done((bf16[16,128,1024]{2,1,0:T(8,128)(2,1)S(1)}, bf16[16,128,1024]{2,1,0:T(8,128)(2,1)}, u32[]{:S(2)}) %copy-start) | copy-done | bytes 4194328
  65.2 0.0 copy-start.4
  65.3 56.6 %shard_map.120 = bf16[128,1152]{1,0:T(8,128)(2,1)S(1)} custom-call(bf16[16,128,1024]{2,1,0:T(8,128)(2,1)S(1)} %copy-done, bf16[16,128,128]{2,1,0:T(8,128)(2,1)S(1)} %get-tuple-element.12.refs_1_), custom_call_target="tpu_custom_call" | custom-call | tf_op jit(solution)/shard_map/pallas_call | solution.py:317
  121.9 0.1 copy.29
  121.9 0.8 slice.12
  122.7 0.0 copy-done.4
  122.7 0.6 select_reduce_fusion
  123.3 0.0 copy-start.5
  123.3 0.0 copy-start.6
  123.3 6.1 %fusion.18 = bf16[1,1024,384]{2,1,0:T(8,128)(2,1)} fusion(bf16[2048,384]{1,0:T(8,128)(2,1)} %bitcast.25, bf16[2048,2176]{1,0:T(8,128)(2,1)} %bitcast.21), kind=kOutput, calls=%fused_computation.10 | convolution fusion | flops 1611005952 | bytes 6553600 | tf_op jit(solution)/shard_map/dot_general | solution.py:374
  129.4 0.0 copy-done.5
  129.4 0.0 copy-done.6
  129.4 2.7 %fusion.15 = bf16[1,384,1024]{2,1,0:T(8,128)(2,1)} fusion(bf16[2048,384]{1,0:T(8,128)(2,1)S(1)} %bitcast.24, bf16[2048,2176]{1,0:T(8,128)(2,1)S(1)} %bitcast.22), kind=kOutput, calls=%fused_computation.9 | convolution fusion | flops 1611005952 | bytes 6553600 | tf_op jit(solution)/shard_map/dot_general | solution.py:375
  132.1 3.3 %fusion.21 = bf16[1,1024,384]{2,1,0:T(8,128)(2,1)} fusion(bf16[2048,384]{1,0:T(8,128)(2,1)S(1)} %bitcast.20, bf16[2048,2176]{1,0:T(8,128)(2,1)S(1)} %bitcast.23), kind=kOutput, calls=%fused_computation.11 | convolution fusion | flops 1611005952 | bytes 6553600 | tf_op jit(solution)/shard_map/dot_general | solution.py:373
  (2 shorter events, 0.0 us)
Async XLA Ops:
  0.6 4.5 %copy-start.2 = (bf16[1,1024,384]{2,1,0:T(8,128)(2,1)S(1)}, bf16[1,1024,384]{2,1,0:T(8,128)(2,1)}, u32[]{:S(2)}) copy-start(bf16[1,1024,384]{2,1,0:T(8,128)(2,1)} %param.14) | copy-start | bytes 2359300
  0.6 4.5 %copy-start.1 = (bf16[1,1024,384]{2,1,0:T(8,128)(2,1)S(1)}, bf16[1,1024,384]{2,1,0:T(8,128)(2,1)}, u32[]{:S(2)}) copy-start(bf16[1,1024,384]{2,1,0:T(8,128)(2,1)} %param.13) | copy-start | bytes 2359300
  5.1 1.1 copy-start.3
  63.1 2.2 %copy-start = (bf16[16,128,1024]{2,1,0:T(8,128)(2,1)S(1)}, bf16[16,128,1024]{2,1,0:T(8,128)(2,1)}, u32[]{:S(2)}) copy-start(bf16[16,128,1024]{2,1,0:T(8,128)(2,1)} %get-tuple-element.11.refs_0_) | copy-start | bytes 12582916
  65.2 57.5 %copy-start.4 = (s32[128,8]{0,1:T(8,128)S(1)}, s32[128,8]{0,1:T(8,128)}, u32[]{:S(2)}) copy-start(s32[128,8]{0,1:T(8,128)} %param.11) | copy-start | bytes 12292
  123.3 6.1 %copy-start.5 = (bf16[16,128,2176]{2,1,0:T(8,128)(2,1)S(1)}, bf16[16,128,2176]{2,1,0:T(8,128)(2,1)}, u32[]{:S(2)}) copy-start(bf16[16,128,2176]{2,1,0:T(8,128)(2,1)} %get-tuple-element.13) | copy-start | bytes 26738692
  123.3 6.1 %copy-start.6 = (bf16[16,128,384]{2,1,0:T(8,128)(2,1)S(1)}, bf16[16,128,384]{2,1,0:T(8,128)(2,1)}, u32[]{:S(2)}) copy-start(bf16[16,128,384]{2,1,0:T(8,128)(2,1)} %get-tuple-element.16) | copy-start | bytes 4718596
where the time goes:
time: 136 us; the launch traced here: 135 us
  Pallas kernels  113 us (83%)
  matrix products  12.2 us (9%)
  other arithmetic  4.64 us (3%)
  local copies, waits for them, and re-layouts  4.36 us (3%)
    pallas_call x1, Pallas kernels, gather_rows(): pl.pallas_call(lambda *refs: gather_kernel(depth, split, *refs), out_shap...  56.8 us
    pallas_call x1, Pallas kernels, scatter_rows(): pl.pallas_call(lambda *refs: scatter_kernel(depth, split, *refs), out_sha...  56.6 us
    dot_general x1, matrix products, weight_grads(): lax.dot_general(x, db, contract_rows, preferred_element_type=jnp.float32)  6.08 us
    unnamed x14, local copies, waits for them, and re-layouts  3.33 us
    dot_general x1, matrix products, weight_grads(): lax.dot_general(x, da, contract_rows, preferred_element_type=jnp.float32)  3.25 us

commit v1 on v0

v1 whole, which is shorter than its diff:
```python
import jax
import jax.numpy as jnp
from jax import lax
from jax.experimental import pallas as pl
from jax.experimental.pallas import tpu as pltpu
from jax.sharding import PartitionSpec as P

TOP = 8
ROWS_PER_CHUNK = 4096

contract_rows = (((0,), (0,)), ((), ()))
contract_cols = (((1,), (1,)), ((), ()))

MESH = pl.DeviceIdType.MESH
VMEM_GRANT = 58 * 2**20


def place(depth):
    me = lax.axis_index("expert")
    z, y, c = me // 4, (me // 2) % 2, me % 2
    return me, z, y, c, depth - 1


def index_of(z, y, c):
    return (z * 2 + y) * 2 + c


def greet(me, devices):
    sem = pltpu.get_barrier_semaphore()
    for peer in range(devices):
        pl.when(peer != me)(
            lambda peer=peer: pl.semaphore_signal(
                sem, inc=1, device_id={"expert": peer}, device_id_type=MESH
            )
        )
    pl.semaphore_wait(sem, devices - 1)


class Sender:
    def __init__(self, sems):
        self.sems = sems

    def send(self, group, cond, make):
        if cond is None:
            make(self.sems.at[group]).start()
        else:
            pl.when(cond)(lambda: make(self.sems.at[group]).start())

    def sent(self, group, ref):
        pltpu.make_async_copy(ref, ref, self.sems.at[group]).wait()


def remote(src, dst, recv_sem, peer):
    return lambda send_sem: pltpu.make_async_remote_copy(
        src_ref=src(), dst_ref=dst(), send_sem=send_sem, recv_sem=recv_sem(),
        device_id={"expert": peer()}, device_id_type=MESH,
    )


def landed(ref, sem):
    pltpu.make_async_copy(ref, ref, sem).wait()


TUNED_DEPTH = 4
TUNED_SHARES = (32, 32, 16, 16, 16, 16)
TUNED = [
    ("own", 0), ("own", 1), ("relay", 0, 1), ("relay", 0, -1), ("own", 3), ("relay", 0, 2),
    ("relay", 0, -2), ("cross", 0, 0), ("own", 2), ("relay", 0, 3), ("relay", 0, -3),
    ("relay", 1, -1), ("cross", 0, -3), ("relay", 1, 1), ("relay", 1, -2), ("cross", 0, 1),
    ("cross", 0, -1), ("gates", 0), ("cross", 0, 3), ("relay", 1, 2), ("cross", 0, -2),
    ("cross", 0, 2), ("cross", 3, 0), ("relay", 1, 3), ("finish", 0), ("relay", 2, 1),
    ("relay", 1, -3), ("own", 4), ("relay", 2, -1), ("relay", 3, 1), ("fwd", 0, 0),
    ("relay", 2, 2), ("own", 5), ("relay", 2, -2), ("cross", 1, 1), ("relay", 3, -1),
    ("fwd", 0, 1), ("relay", 4, -1), ("cross", 1, -2), ("relay", 3, 2), ("cross", 1, -3),
    ("cross", 1, -1), ("cross", 1, 0), ("relay", 2, 3), ("cross", 1, 2), ("sc", 0, 0),
    ("cross", 1, 3), ("relay", 2, -3), ("relay", 4, -2), ("relay", 3, -2), ("relay", 3, 3),
    ("relay", 4, 1), ("relay", 5, 1), ("sc", 0, 1), ("finish", 1), ("cross", 2, 1),
    ("relay", 5, -1), ("fwd", 1, 0), ("cross", 2, -1), ("relay", 4, 2), ("fwd", 1, 1),
    ("sc", 0, 2), ("cross", 2, 0), ("wg", 0, 1), ("relay", 5, 2), ("wg", 1, 1), ("cross", 2, 2),
    ("sc", 1, 0), ("cross", 2, -3), ("relay", 5, -2), ("cross", 2, 3), ("cross", 2, -2),
    ("wg", 0, 0), ("relay", 4, 3), ("sc", 1, 1), ("finish", 2), ("fwd", 2, 0), ("wg", 2, 1),
    ("relay", 3, -3), ("relay", 4, -3), ("cross", 3, 1), ("wg", 1, 0), ("cross", 3, -2),
    ("cross", 3, -1), ("cross", 4, -1), ("sc", 2, 0), ("cross", 5, 1), ("sc", 2, 1),
    ("cross", 3, 2), ("cross", 4, -2), ("cross", 3, 3), ("wg", 2, 0), ("cross", 4, 1),
    ("cross", 3, -3), ("sc", 1, 2), ("cross", 4, 2), ("relay", 5, -3), ("cross", 5, 0),
    ("relay", 5, 3), ("cross", 5, -2), ("cross", 5, -1), ("cross", 4, -3), ("finish", 3),
    ("cross", 4, 0), ("cross", 4, 3), ("fwd", 3, 0), ("sc", 2, 2), ("finish", 4),
    ("cross", 5, -3), ("cross", 5, 3), ("cross", 5, 2), ("fwd", 4, 0), ("sc", 3, 0), ("wg", 3, 1),
    ("finish", 5), ("wg", 3, 0), ("sc", 3, 1), ("fwd", 5, 0), ("sc", 4, 0), ("sc", 4, 1),
    ("sc", 5, 0), ("sc", 2, 3), ("sc", 3, 2), ("sc", 1, 3), ("sc", 5, 1), ("wg", 4, 0),
    ("wg", 4, 1), ("sc", 4, 2), ("ggout", 0), ("sc", 0, 3), ("sc", 5, 2), ("sc", 3, 3),
    ("sc", 4, 3), ("ggin", 0), ("sc", 5, 3), ("wg", 5, 1), ("total", 0), ("total", 2),
    ("total", 1), ("total", 4), ("total", 3), ("wg", 5, 0), ("total", 5),
]


def row_chunks(tok):
    whole = sum(TUNED_SHARES)
    sizes = [tok * share // whole for share in TUNED_SHARES]
    return [(sum(sizes[:k]), size) for k, size in enumerate(sizes)]


def step_order(depth, n):
    if depth == TUNED_DEPTH:
        return TUNED
    steps = [("own", 0), ("gates", 0)]
    for k in range(n):
        steps += [("own", k)] if k else []
        for d in range(1, depth):
            steps += [("relay", k, -d), ("relay", k, d)]
        steps += [("cross", k, d) for d in range(1 - depth, depth)]
        steps += [("finish", k), ("fwd", k, 0), ("fwd", k, 1), ("wg", k, 0), ("wg", k, 1)]
        steps += [("sc", k, p) for p in range(depth)] + [("total", k)]
    return steps + [("ggout", 0), ("ggin", 0)]


def fused_kernel(
    depth, order, home_cap, rep_cap,
    x_hbm, dy_hbm, gates_hbm, ids_hbm, table_hbm, wg_hbm, wu_hbm, wd_hbm,
    out_ref, ggo_ref, dwg_ref, dwu_ref, dwd_ref,
    buf, gbuf, gcol, ggcol, ggs, ggr, w1, wd, dadb, hgb, acc1, acc2, dx, rc, rzu, rzd, ysend, ry,
    gates_ref, ids_ref, table_ref,
    local_sems, send_sems, recv_sems, pair_sems, gate_sem, gg_sem, twin_sems, up_sems, down_sems,
    y_sems,
):
    f32, bf16 = jnp.float32, jnp.bfloat16
    devices = 4 * depth
    me, z, y, c, last = place(depth)
    tok, width = x_hbm.shape
    hidden = wd_hbm.shape[0]
    chunks = row_chunks(tok)
    lanes = gcol.shape[1]

    def local(src, dst, i):
        return pltpu.make_async_copy(src, dst, local_sems.at[i])

    own_copies = [local(x_hbm, buf.at[me, 0], 0), local(dy_hbm, buf.at[me, 1], 1)]
    weight_copies = [
        local(wg_hbm, w1.at[:, pl.ds(0, hidden)], 2),
        local(wu_hbm, w1.at[:, pl.ds(hidden, hidden)], 3),
        local(wd_hbm, wd, 4),
    ]
    plan_copies = [
        local(gates_hbm, gates_ref, 5), local(ids_hbm, ids_ref, 6), local(table_hbm, table_ref, 7),
    ]
    for copy in own_copies + plan_copies + weight_copies:
        copy.start()
    greet(me, devices)
    for copy in own_copies:
        copy.wait()

    out = Sender(send_sems)
    up = lambda: index_of(z + 1, y, c)
    down = lambda: index_of(z - 1, y, c)
    over = lambda: index_of(z, 1 - y, c)
    twin = lambda: index_of(z, y, 1 - c)
    can_up, can_down = z < last, z > 0
    half = depth // 2

    def rows_of(k):
        return pl.ds(*chunks[k])

    OWN, PASS, PAIR, CHAIN, HOME, GATE, BACK = range(7)

    def push(group, cond, b, k, peer):
        block = lambda: buf.at[b(), :, rows_of(k)]
        sem = (lambda: pair_sems.at[k]) if peer is twin else (lambda: recv_sems.at[k, b()])
        out.send(group, cond, remote(block, block, sem, peer))

    def arrived(k, b):
        landed(buf.at[b, :, rows_of(k)], recv_sems.at[k, b])

    def own(k):
        mine = lambda: me
        push(OWN, None, mine, k, over)
        push(OWN, can_up, mine, k, up)
        push(OWN, can_down, mine, k, down)
        push(OWN, None, mine, k, twin)

    def relay(k, off):
        cond = z + off >= 0 if off < 0 else z + off <= last
        more, onward = (can_up, up) if off < 0 else (can_down, down)
        b = lambda: index_of(z + off, y, c)
        pl.when(cond)(lambda: arrived(k, b()))
        if abs(off) < depth - 1:
            push(PASS, cond & more, b, k, onward)
        push(PASS, cond, b, k, over)
        push(PASS, cond, b, k, twin)

    def cross(k, off):
        b = lambda: index_of(z + off, 1 - y, c)
        cond = None if off == 0 else z + off >= 0 if off < 0 else z + off <= last
        if cond is None:
            arrived(k, b())
        else:
            pl.when(cond)(lambda: arrived(k, b()))
        push(PASS, cond, b, k, twin)

    def finish(k):
        landed(buf.at[pl.ds(0, devices // 2), :, rows_of(k)], pair_sems.at[k])

    lane = lax.broadcasted_iota(jnp.int32, (tok, lanes), 1)
    expert = lax.broadcasted_iota(jnp.int32, (devices, tok), 0)

    def send_gates():
        copies = jnp.ones((devices, tok), f32)
        for d in range(devices):
            copies = copies + jnp.where(expert == table_ref[d], 1.0, 0.0)
        dense = jnp.zeros((devices, tok), f32)
        named = jnp.zeros((devices, tok), f32)
        for k in range(ids_ref.shape[0]):
            hot = ids_ref[k : k + 1] == expert
            dense = jnp.where(hot, gates_ref[k : k + 1].astype(f32), dense)
            named = jnp.where(hot, 1.0, named)
        row = lax.broadcasted_iota(jnp.int32, (tok, tok), 0)
        col = lax.broadcasted_iota(jnp.int32, (tok, tok), 1)
        earlier = jnp.where(row < col, 1.0, 0.0).astype(bf16)
        rank = jnp.dot(named.astype(bf16), earlier, preferred_element_type=f32)
        position = jnp.floor((rank + 0.5) / copies)
        turn = rank + me.astype(f32)
        copy_index = turn - copies * jnp.floor((turn + 0.5) / copies)
        limit = jnp.where(copy_index < 0.5, float(home_cap), float(rep_cap))
        gbuf[me] = jnp.where((named > 0.5) & (position < limit), dense, 0.0).astype(bf16)
        for peer in range(devices):
            out.send(
                GATE, peer != me,
                remote(
                    lambda: gbuf.at[me], lambda: gbuf.at[me], lambda: gate_sem,
                    lambda peer=peer: peer,
                ),
            )

    def take_gates():
        landed(gbuf.at[pl.ds(0, devices - 1)], gate_sem)
        flat = gbuf[...].reshape(devices * devices, tok)
        r = lax.broadcasted_iota(jnp.int32, (devices * devices, lanes), 0)
        l = lax.broadcasted_iota(jnp.int32, (devices * devices, lanes), 1)
        pick = jnp.where(r == l * devices + me, 1.0, 0.0).astype(bf16)
        gcol[...] = lax.dot_general(flat, pick, contract_rows, preferred_element_type=f32)
        ggcol[...] = jnp.zeros_like(ggcol)

    def units(k):
        if chunks[k][1] * devices <= 256 or depth % 2:
            return [(0, depth)]
        first = jnp.where(z < half, half, 0)
        return [(first, half), (half - first, half)]

    def forward(k, u):
        if u >= len(units(k)):
            return
        r0, size = chunks[k]
        p0, planes = units(k)[u]
        nb = planes * 4
        at = pl.ds(p0 * 4, nb)
        rows = pl.ds(r0, size)
        x = buf[at, 0, rows, :].reshape(nb * size, width)
        dy = buf[at, 1, rows, :].reshape(nb * size, width)
        g = gcol[rows, :]
        spot = lane[:size]
        gate = jnp.concatenate(
            [
                jnp.sum(jnp.where(spot == p0 * 4 + j, g, 0.0), axis=1, keepdims=True)
                for j in range(nb)
            ],
            axis=0,
        )
        ab = jnp.dot(x, w1[...], preferred_element_type=f32)
        a, b = ab[:, :hidden], ab[:, hidden:]
        v = lax.dot_general(dy, wd[...], contract_cols, preferred_element_type=f32)
        sig = jax.nn.sigmoid(a)
        act = a * sig
        product = act * b
        gate_grad = jnp.sum(product.astype(bf16).astype(f32) * v, axis=1, keepdims=True)
        gate_grad = jnp.where(gate > 0, gate_grad, 0.0)
        gu = gate * v
        da = (gu * b * sig * (1.0 + a * (1.0 - sig))).astype(bf16)
        db = (gu * act).astype(bf16)
        both_grads = jnp.concatenate([da, db], axis=1)
        hgb[k % 2, at, pl.ds(0, size), :] = (gate * product).astype(bf16).reshape(nb, size, hidden)
        dadb[k % 2, at, pl.ds(0, size), :] = both_grads.reshape(nb, size, 2 * hidden)
        back = lax.dot_general(both_grads, w1[...], contract_cols, preferred_element_type=f32)
        dx[pl.ds(p0, planes), :, :, rows, :] = back.astype(bf16).reshape(
            planes, 2, 2, size, width
        )
        held = ggcol[rows, :]
        for j in range(nb):
            held = jnp.where(spot == p0 * 4 + j, gate_grad[j * size : (j + 1) * size], held)
        ggcol[rows, :] = held
        src = lambda: dx.at[pl.ds(p0, planes), :, 1 - c, rows, :]
        dst = lambda: rc.at[pl.ds(p0, planes), :, rows, :]
        out.send(PAIR, None, remote(src, dst, lambda: twin_sems.at[k, u], twin))

    def twin_sums(k):
        for u, (p0, planes) in enumerate(units(k)):
            landed(rc.at[pl.ds(p0, planes), :, rows_of(k), :], twin_sems.at[k, u])

    tile = 256 if width % 256 == 0 else 128

    def weight_tile(k, j, which):
        size = chunks[k][1]
        rows = rows_of(k)
        cols = pl.ds(j * tile, tile)
        first, final = k == 0, k == len(chunks) - 1
        if which == 0:
            x = buf[:, 0, rows, cols].reshape(devices * size, tile)
            d = dadb[k % 2, :, pl.ds(0, size), :].reshape(devices * size, 2 * hidden)
            v = lax.dot_general(x, d, contract_rows, preferred_element_type=f32)
            if not first:
                v = v + acc1[cols, :]
            if final:
                dwg_ref[cols, :] = v[:, :hidden].astype(bf16)
                dwu_ref[cols, :] = v[:, hidden:].astype(bf16)
            else:
                acc1[cols, :] = v
        else:
            dy = buf[:, 1, rows, cols].reshape(devices * size, tile)
            h = hgb[k % 2, :, pl.ds(0, size), :].reshape(devices * size, hidden)
            v = lax.dot_general(h, dy, contract_rows, preferred_element_type=f32)
            if not first:
                v = v + acc2[:, cols]
            if final:
                dwd_ref[:, cols] = v.astype(bf16)
            else:
                acc2[:, cols] = v

    def weights(k, which):
        for j in range(width // tile):
            weight_tile(k, j, which)

    def part_sum(zz, yy, rows, extra):
        total = dx[zz, yy, c, rows, :].astype(f32) + rc[zz, yy, rows, :].astype(f32)
        for ref in extra:
            total = total + ref[zz, yy, rows, :].astype(f32)
        return total

    def chain(k, p):
        rows = rows_of(k)
        for way, there, zz_of, ref, sems, has, peer in (
            (0, z <= p, lambda: z + last - p, rzu, up_sems, z > 0, up),
            (1, last - z <= p, lambda: z + p - last, rzd, down_sems, z < last, down),
        ):

            def step():
                zz = zz_of()
                pl.when(has)(lambda: landed(ref.at[zz, :, rows, :], sems.at[k, zz]))
                for yy in range(2):
                    ref[zz, yy, rows, :] = part_sum(zz, yy, rows, (ref,)).astype(bf16)

            pl.when(there)(step)
            out.send(
                CHAIN, there,
                remote(
                    lambda: ref.at[zz_of(), :, rows, :], lambda: ref.at[zz_of(), :, rows, :],
                    lambda: sems.at[k, zz_of()], peer,
                ),
            )

    def home(k):
        rows = rows_of(k)
        pl.when(z > 0)(lambda: landed(rzu.at[z, :, rows, :], up_sems.at[k, z]))
        pl.when(z < last)(lambda: landed(rzd.at[z, :, rows, :], down_sems.at[k, z]))
        ysend[rows, :] = part_sum(z, 1 - y, rows, (rzu, rzd)).astype(bf16)
        out.send(
            HOME, None,
            remote(
                lambda: ysend.at[rows, :], lambda: ry.at[rows, :], lambda: y_sems.at[k], over
            ),
        )

    def total(k):
        rows = rows_of(k)
        mine = part_sum(z, y, rows, (rzu, rzd))
        landed(ry.at[rows, :], y_sems.at[k])
        out_ref[rows, :] = (mine + ry[rows, :].astype(f32)).astype(bf16)

    def scatter_point(k, p):
        if p == 0:
            twin_sums(k)
        if p < last:
            chain(k, p)
        else:
            home(k)

    def send_gate_grads():
        turned = ggcol[...].T
        for b in range(devices):
            ggs[b] = turned[b : b + 1]
        ggr[me] = ggs[me]
        for peer in range(devices):
            out.send(
                BACK, peer != me,
                remote(
                    lambda peer=peer: ggs.at[peer], lambda: ggr.at[me], lambda: gg_sem,
                    lambda peer=peer: peer,
                ),
            )

    def take_gate_grads():
        landed(ggr.at[pl.ds(0, devices - 1)], gg_sem)
        held = ggr[...].reshape(devices, tok)
        for k in range(ids_ref.shape[0]):
            hot = ids_ref[k : k + 1] == expert
            picked = jnp.sum(jnp.where(hot, held, 0.0), axis=0, keepdims=True)
            ggo_ref[k : k + 1] = picked.astype(bf16)

    def gates_out(k):
        for copy in plan_copies:
            copy.wait()
        send_gates()

        @pl.when(z == 0)
        def _():
            rzu[...] = jnp.zeros_like(rzu)

        @pl.when(z == last)
        def _():
            rzd[...] = jnp.zeros_like(rzd)

    def ready(k):
        finish(k)
        if k == 0:
            take_gates()
            for copy in weight_copies:
                copy.wait()

    steps = dict(
        own=own, gates=gates_out, relay=relay, cross=cross, finish=ready, fwd=forward,
        wg=weights, sc=scatter_point, total=total, ggout=lambda k: send_gate_grads(),
        ggin=lambda k: take_gate_grads(),
    )
    for name, *rest in order:
        steps[name](*rest)

    def sent_blocks(zz):
        ends = (zz < last) + (zz > 0)
        passed = depth
        for off in range(1, depth):
            passed += (zz >= off) * (2 + (zz < last and off < last))
            passed += (zz + off <= last) * (2 + (zz > 0 and off < last))
        out.sent(OWN, buf.at[pl.ds(0, 2 + ends)])
        out.sent(PASS, buf.at[pl.ds(0, passed)])

    for zz in range(depth):
        pl.when(z == zz)(lambda: sent_blocks(zz))
    out.sent(PAIR, rc)
    if depth > 1:
        out.sent(CHAIN, rzu.at[pl.ds(0, depth - 1)])
    out.sent(HOME, ysend)
    out.sent(GATE, gbuf.at[pl.ds(0, devices - 1)])
    out.sent(BACK, ggs.at[pl.ds(0, devices - 1)])


def fused_grads(x, dy, gates, ids, table, gate_w, up_w, down_w, devices, home_cap, rep_cap):
    depth = devices // 4
    tok, width = x.shape
    hidden = down_w.shape[0]
    f32, bf16 = jnp.float32, jnp.bfloat16
    n = len(row_chunks(tok))
    most = max(size for _, size in row_chunks(tok))
    vmem, dma = pltpu.VMEM, pltpu.SemaphoreType.DMA
    whole = pl.BlockSpec(memory_space=pltpu.VMEM)
    hbm = pl.BlockSpec(memory_space=pltpu.HBM)
    shape = jax.ShapeDtypeStruct
    outs = pl.pallas_call(
        lambda *refs: fused_kernel(depth, step_order(depth, n), home_cap, rep_cap, *refs),
        out_shape=[
            shape((tok, width), bf16), shape(gates.shape, bf16), shape(gate_w.shape, bf16),
            shape(up_w.shape, bf16), shape(down_w.shape, bf16),
        ],
        in_specs=[hbm] * 8,
        out_specs=[whole] * 5,
        scratch_shapes=[
            vmem((devices, 2, tok, width), bf16), vmem((devices, devices, tok), bf16),
            vmem((tok, 128), f32), vmem((tok, 128), f32),
            vmem((devices, 1, tok), f32), vmem((devices, 1, tok), f32),
            vmem((width, 2 * hidden), bf16), vmem((hidden, width), bf16),
            vmem((2, devices, most, 2 * hidden), bf16), vmem((2, devices, most, hidden), bf16),
            vmem((width, 2 * hidden), f32), vmem((hidden, width), f32),
            vmem((depth, 2, 2, tok, width), bf16), vmem((depth, 2, tok, width), bf16),
            vmem((depth, 2, tok, width), bf16), vmem((depth, 2, tok, width), bf16),
            vmem((tok, width), bf16), vmem((tok, width), bf16),
            vmem(gates.shape, bf16), vmem(ids.shape, ids.dtype),
            pltpu.SMEM(table.shape, table.dtype),
            dma((8,)), dma((7,)), dma((n, devices)), dma((n,)), dma, dma,
            dma((n, 2)), dma((n, depth)), dma((n, depth)), dma((n,)),
        ],
        compiler_params=pltpu.CompilerParams(
            collective_id=0, has_side_effects=True, vmem_limit_bytes=VMEM_GRANT
        ),
    )(x, dy, gates, ids, table, gate_w, up_w, down_w)
    return store_all(outs)


def store_kernel(n, *refs):
    sems = refs[2 * n]
    copies = [
        pltpu.make_async_copy(refs[i], refs[n + i], sems.at[i]) for i in range(n)
    ]
    for copy in copies:
        copy.start()
    for copy in copies:
        copy.wait()


def store_all(arrays):
    n = len(arrays)
    return pl.pallas_call(
        lambda *refs: store_kernel(n, *refs),
        out_shape=[jax.ShapeDtypeStruct(v.shape, v.dtype) for v in arrays],
        in_specs=[pl.BlockSpec(memory_space=pltpu.VMEM)] * n,
        out_specs=[pl.BlockSpec(memory_space=pltpu.HBM)] * n,
        scratch_shapes=[pltpu.SemaphoreType.DMA((n,))],
    )(*arrays)


def keep_plan(gates, row_ids, replica_table, source, devices, home_cap, rep_cap):
    tok = row_ids.shape[0]
    experts = jnp.arange(devices, dtype=jnp.int32)
    hot = row_ids[:, :, None] == experts[None, None, :]
    named = jnp.any(hot, axis=1)
    dense_gate = jnp.sum(jnp.where(hot, gates.astype(jnp.float32)[:, :, None], 0.0), axis=1)
    copies = 1 + jnp.sum((replica_table[:, None] == experts[None, :]).astype(jnp.int32), axis=0)
    order = jnp.arange(tok, dtype=jnp.int32)
    earlier = (order[:, None] > order[None, :]).astype(jnp.bfloat16)
    rank = jnp.dot(earlier, named.astype(jnp.bfloat16), preferred_element_type=jnp.float32)
    many = copies.astype(jnp.float32)[None, :]
    position = jnp.floor((rank + 0.5) / many)
    turn = rank + source.astype(jnp.float32)
    copy_index = turn - many * jnp.floor((turn + 0.5) / many)
    limit = jnp.where(copy_index < 0.5, float(home_cap), float(rep_cap))
    kept = named & (position < limit)
    return jnp.where(kept, dense_gate, 0.0).astype(jnp.bfloat16)


def row_grads(x, dy, gate, gate_w, up_w, down_w):
    a = jnp.dot(x, gate_w, preferred_element_type=jnp.float32)
    b = jnp.dot(x, up_w, preferred_element_type=jnp.float32)
    u = lax.dot_general(dy, down_w, contract_cols, preferred_element_type=jnp.float32)
    sig = jax.nn.sigmoid(a)
    act = a * sig
    product = act * b
    hidden = product.astype(jnp.bfloat16).astype(jnp.float32)
    gate_grad = jnp.sum(hidden * u, axis=1, keepdims=True)
    gate_grad = jnp.where(gate > 0, gate_grad, 0.0)
    hg = (gate * product).astype(jnp.bfloat16)
    gu = gate * u
    da = (gu * b * sig * (1.0 + a * (1.0 - sig))).astype(jnp.bfloat16)
    db = (gu * act).astype(jnp.bfloat16)
    dx = lax.dot_general(da, gate_w, contract_cols, preferred_element_type=jnp.float32)
    dx = dx + lax.dot_general(db, up_w, contract_cols, preferred_element_type=jnp.float32)
    return gate_grad, hg, da, db, dx


def weight_grads(x, dy, hg, da, db):
    dwg = lax.dot_general(x, da, contract_rows, preferred_element_type=jnp.float32)
    dwu = lax.dot_general(x, db, contract_rows, preferred_element_type=jnp.float32)
    dwd = lax.dot_general(hg, dy, contract_rows, preferred_element_type=jnp.float32)
    return dwg, dwu, dwd


def on_device(tokens_in, grad_out, gates, expert_ids, replica_table, w_gate, w_up, w_down):
    devices = lax.axis_size("expert")
    me = lax.axis_index("expert")
    tok, width = tokens_in.shape
    home_cap = max(2, 5 * tok * TOP // (4 * devices))
    rep_cap = max(2, tok * TOP // (2 * devices))
    if devices * tok <= ROWS_PER_CHUNK and devices % 16 == 0 and devices <= 128 and tok % 128 == 0:
        outs = fused_grads(
            tokens_in, grad_out, gates.T, expert_ids.T, replica_table, w_gate[0], w_up[0], w_down[0],
            devices, home_cap, rep_cap,
        )
        return (outs[0], outs[1].T, *[g[None] for g in outs[2:]])
    kept_gate = keep_plan(gates, expert_ids, replica_table, me, devices, home_cap, rep_cap)
    lanes = -(-devices // 128) * 128
    kept_gate = jnp.pad(kept_gate, ((0, 0), (0, lanes - devices)))
    payload = jnp.concatenate([tokens_in, grad_out, kept_gate], axis=1)
    chunks = max(1, devices * tok // ROWS_PER_CHUNK)
    part = tok // chunks
    mine = jnp.arange(lanes, dtype=jnp.int32)[None, :] == me
    backs, sums = [], None
    for c in range(chunks):
        rows = lax.all_gather(payload[c * part : (c + 1) * part], "expert", axis=0, tiled=True)
        gate = jnp.sum(
            jnp.where(mine, rows[:, 2 * width :].astype(jnp.float32), 0.0),
            axis=1,
            keepdims=True,
        )
        gate_grad, hg, da, db, dx = row_grads(
            rows[:, :width], rows[:, width : 2 * width], gate, w_gate[0], w_up[0], w_down[0]
        )
        spread = jnp.where(mine, gate_grad, 0.0).astype(jnp.bfloat16)
        back = jnp.concatenate([dx.astype(jnp.bfloat16), spread], axis=1)
        backs.append(lax.psum_scatter(back, "expert", scatter_dimension=0, tiled=True))
        grads = weight_grads(rows[:, :width], rows[:, width : 2 * width], hg, da, db)
        sums = grads if sums is None else [p + q for p, q in zip(sums, grads)]
        if c + 1 < chunks:
            payload, sums = lax.optimization_barrier((payload, sums))
    back = jnp.concatenate(backs, axis=0)
    experts = jnp.arange(devices, dtype=jnp.int32)
    hot = expert_ids[:, :, None] == experts[None, None, :]
    picked = jnp.where(hot, back[:, None, width : width + devices].astype(jnp.float32), 0.0)
    grad_gates = jnp.sum(picked, axis=2).astype(jnp.bfloat16)
    return (back[:, :width], grad_gates, *[g.astype(jnp.bfloat16)[None] for g in sums])


def solution(mesh):
    return jax.shard_map(
        on_device,
        mesh=mesh,
        in_specs=(
            P(("groups", "expert"), None),
            P(("groups", "expert"), None),
            P(("groups", "expert"), None),
            P(("groups", "expert"), None),
            P("groups"),
            P("expert", None, None),
            P("expert", None, None),
            P("expert", None, None),
        ),
        out_specs=(
            P(("groups", "expert"), None),
            P(("groups", "expert"), None),
            P(("groups", "expert"), None, None),
            P(("groups", "expert"), None, None),
            P(("groups", "expert"), None, None),
        ),
        check_vma=False,
    )
```

time: 136 us -> 88.9 us (0.65)
  the two profiles are of different devices: /device:TPU:10 before, /device:TPU:0 now
where the time goes in v1:
time: 88.9 us; the launch traced here: 88.8 us
  Pallas kernels  88 us (99%)
    pallas_call x1, Pallas kernels, fused_grads(): pl.pallas_call(lambda *refs: fused_kernel(depth, step_order(depth, n), ho...  84.7 us
    pallas_call x1, Pallas kernels, store_all(): pl.pallas_call(lambda *refs: store_kernel(n, *refs), out_shape=[jax.Shape...  3.22 us

profile of v1, /device:TPU:0, one launch (start us, length us, event | category | flops | bytes accessed | tf_op | source)
XLA Modules:
  0.0 88.8 jit_solution(9595246081358442335)
XLA Ops:
  0.6 84.7 %shard_map.119 = (bf16[128,1024]{1,0:T(8,128)(2,1)}, bf16[8,128]{1,0:T(8,128)(2,1)}, bf16[1024,384]{1,0:T(8,128)(2,1)}, bf16[1024,384]{1,0:T(8,128)(2,1)}, bf16[384,1024]{1,0:T(8,128)(2,1)}) custom-call(bf16[128,1024]{1,0:T(8,128)(2,1)} %refs_0_.1, bf16[128,1024]{1,0:T(8,128)(2,1)} %refs_1_.1, bf16[8,128]{1,0:T(8,128)(2,1)} %bitcast.13, s32[8,128]{1,0:T(8,128)} %bitcast.12, ...), custom_call_target="tpu_custom_call" | custom-call | tf_op jit(solution)/shard_map/pallas_call | solution.py:464
  85.4 3.2 %shard_map.120 = (bf16[128,1024]{1,0:T(8,128)(2,1)}, bf16[8,128]{1,0:T(8,128)(2,1)}, bf16[1024,384]{1,0:T(8,128)(2,1)}, bf16[1024,384]{1,0:T(8,128)(2,1)}, bf16[384,1024]{1,0:T(8,128)(2,1)}) custom-call(bf16[128,1024]{1,0:T(8,128)(2,1)} %get-tuple-element.15.refs_0_, bf16[8,128]{1,0:T(8,128)(2,1)} %get-tuple-element.16.refs_1_, ...), custom_call_target="tpu_custom_call" | custom-call | tf_op jit(solution)/shard_map/pallas_call | solution.py:507

commit v2 on v1

--- a/solution.py
+++ b/solution.py
@@ -25,15 +25,17 @@
     return (z * 2 + y) * 2 + c
 
 
-def greet(me, devices):
+def greet(z, y, c, last):
     sem = pltpu.get_barrier_semaphore()
-    for peer in range(devices):
-        pl.when(peer != me)(
-            lambda peer=peer: pl.semaphore_signal(
-                sem, inc=1, device_id={"expert": peer}, device_id_type=MESH
-            )
-        )
-    pl.semaphore_wait(sem, devices - 1)
+
+    def hello(peer):
+        pl.semaphore_signal(sem, inc=1, device_id={"expert": peer}, device_id_type=MESH)
+
+    hello(index_of(z, y, 1 - c))
+    hello(index_of(z, 1 - y, c))
+    pl.when(z > 0)(lambda: hello(index_of(z - 1, y, c)))
+    pl.when(z < last)(lambda: hello(index_of(z + 1, y, c)))
+    pl.semaphore_wait(sem, 2 + (z > 0).astype(jnp.int32) + (z < last).astype(jnp.int32))
 
 
 class Sender:
@@ -62,35 +64,42 @@
 
 
 TUNED_DEPTH = 4
-TUNED_SHARES = (32, 32, 16, 16, 16, 16)
+TUNED_SHARES = (32, 16, 16, 16, 16, 16, 16)
+PAIR_FIRST = (False, False, False, True, True, True, True)
+BOTH_COLUMNS = (False, False, False, True, False, False, False)
 TUNED = [
-    ("own", 0), ("own", 1), ("relay", 0, 1), ("relay", 0, -1), ("own", 3), ("relay", 0, 2),
-    ("relay", 0, -2), ("cross", 0, 0), ("own", 2), ("relay", 0, 3), ("relay", 0, -3),
-    ("relay", 1, -1), ("cross", 0, -3), ("relay", 1, 1), ("relay", 1, -2), ("cross", 0, 1),
-    ("cross", 0, -1), ("gates", 0), ("cross", 0, 3), ("relay", 1, 2), ("cross", 0, -2),
-    ("cross", 0, 2), ("cross", 3, 0), ("relay", 1, 3), ("finish", 0), ("relay", 2, 1),
-    ("relay", 1, -3), ("own", 4), ("relay", 2, -1), ("relay", 3, 1), ("fwd", 0, 0),
-    ("relay", 2, 2), ("own", 5), ("relay", 2, -2), ("cross", 1, 1), ("relay", 3, -1),
-    ("fwd", 0, 1), ("relay", 4, -1), ("cross", 1, -2), ("relay", 3, 2), ("cross", 1, -3),
-    ("cross", 1, -1), ("cross", 1, 0), ("relay", 2, 3), ("cross", 1, 2), ("sc", 0, 0),
-    ("cross", 1, 3), ("relay", 2, -3), ("relay", 4, -2), ("relay", 3, -2), ("relay", 3, 3),
-    ("relay", 4, 1), ("relay", 5, 1), ("sc", 0, 1), ("finish", 1), ("cross", 2, 1),
-    ("relay", 5, -1), ("fwd", 1, 0), ("cross", 2, -1), ("relay", 4, 2), ("fwd", 1, 1),
-    ("sc", 0, 2), ("cross", 2, 0), ("wg", 0, 1), ("relay", 5, 2), ("wg", 1, 1), ("cross", 2, 2),
-    ("sc", 1, 0), ("cross", 2, -3), ("relay", 5, -2), ("cross", 2, 3), ("cross", 2, -2),
-    ("wg", 0, 0), ("relay", 4, 3), ("sc", 1, 1), ("finish", 2), ("fwd", 2, 0), ("wg", 2, 1),
-    ("relay", 3, -3), ("relay", 4, -3), ("cross", 3, 1), ("wg", 1, 0), ("cross", 3, -2),
-    ("cross", 3, -1), ("cross", 4, -1), ("sc", 2, 0), ("cross", 5, 1), ("sc", 2, 1),
-    ("cross", 3, 2), ("cross", 4, -2), ("cross", 3, 3), ("wg", 2, 0), ("cross", 4, 1),
-    ("cross", 3, -3), ("sc", 1, 2), ("cross", 4, 2), ("relay", 5, -3), ("cross", 5, 0),
-    ("relay", 5, 3), ("cross", 5, -2), ("cross", 5, -1), ("cross", 4, -3), ("finish", 3),
-    ("cross", 4, 0), ("cross", 4, 3), ("fwd", 3, 0), ("sc", 2, 2), ("finish", 4),
-    ("cross", 5, -3), ("cross", 5, 3), ("cross", 5, 2), ("fwd", 4, 0), ("sc", 3, 0), ("wg", 3, 1),
-    ("finish", 5), ("wg", 3, 0), ("sc", 3, 1), ("fwd", 5, 0), ("sc", 4, 0), ("sc", 4, 1),
-    ("sc", 5, 0), ("sc", 2, 3), ("sc", 3, 2), ("sc", 1, 3), ("sc", 5, 1), ("wg", 4, 0),
-    ("wg", 4, 1), ("sc", 4, 2), ("ggout", 0), ("sc", 0, 3), ("sc", 5, 2), ("sc", 3, 3),
-    ("sc", 4, 3), ("ggin", 0), ("sc", 5, 3), ("wg", 5, 1), ("total", 0), ("total", 2),
-    ("total", 1), ("total", 4), ("total", 3), ("wg", 5, 0), ("total", 5),
+    ("own", 0), ("own", 1), ("gates", 0), ("own", 2), ("relay", 0, 1), ("relay", 0, -1),
+    ("own", 3), ("relay", 1, 1), ("relay", 0, 2), ("relay", 1, -1), ("relay", 1, 2),
+    ("relay", 0, -2), ("relay", 1, -2), ("relay", 0, -3), ("relay", 0, 3), ("relay", 2, -1),
+    ("relay", 2, 1), ("cross", 1, 1), ("cross", 0, 0), ("cross", 1, 0), ("relay", 1, -3),
+    ("relay", 1, 3), ("cross", 2, 0), ("cross", 3, 0), ("cross", 0, 1), ("relay", 2, 2),
+    ("cross", 0, 2), ("cross", 0, -1), ("relay", 2, -2), ("relay", 3, -1), ("own", 4),
+    ("cross", 0, -2), ("relay", 3, 1), ("cross", 0, 3), ("cross", 1, -1), ("relay", 2, 3),
+    ("cross", 0, -3), ("relay", 2, -3), ("own", 5), ("cross", 3, 1), ("cross", 3, -1),
+    ("cross", 1, -2), ("own", 6), ("finish", 0), ("fwd", 0, 0), ("fwd", 0, 1), ("trade", 0),
+    ("cross", 1, 2), ("cross", 1, 3), ("cross", 2, -1), ("relay", 4, 1), ("relay", 5, 1),
+    ("relay", 4, -1), ("wg", 0, 1), ("cross", 1, -3), ("cross", 2, 1), ("wg", 0, 0),
+    ("cross", 4, 0), ("relay", 3, -2), ("relay", 5, -1), ("cross", 2, -2), ("cross", 2, 2),
+    ("cross", 3, 2), ("sc", 0, 0), ("finish", 1), ("cross", 2, 3), ("cross", 2, -3),
+    ("fwd", 1, 0), ("cross", 3, -2), ("relay", 3, 2), ("finish", 2), ("relay", 4, 2),
+    ("relay", 4, -2), ("fwd", 2, 0), ("wg", 1, 0), ("relay", 5, 2), ("trade", 1), ("cross", 5, 0),
+    ("cross", 6, 0), ("relay", 3, -3), ("relay", 5, -2), ("cross", 3, 3), ("relay", 6, 1),
+    ("cross", 4, 1), ("wg", 1, 1), ("relay", 6, -1), ("sc", 0, 1), ("cross", 3, -3), ("sc", 1, 0),
+    ("relay", 3, 3), ("wg", 2, 1), ("trade", 2), ("wg", 2, 0), ("relay", 4, 3), ("cross", 4, -1),
+    ("relay", 4, -3), ("finish", 3), ("fwd", 3, 0), ("relay", 5, 3), ("relay", 5, -3),
+    ("wg", 3, 1), ("sc", 2, 0), ("relay", 6, -2), ("relay", 6, 2), ("sc", 0, 2), ("cross", 4, -3),
+    ("cross", 4, 3), ("cross", 4, -2), ("cross", 5, -1), ("sc", 1, 1), ("cross", 4, 2),
+    ("cross", 5, 2), ("wg", 3, 0), ("cross", 5, 1), ("cross", 6, 1), ("cross", 5, -2),
+    ("cross", 6, -1), ("relay", 6, 3), ("relay", 6, -3), ("trade", 3), ("cross", 5, 3),
+    ("cross", 5, -3), ("finish", 4), ("fwd", 4, 0), ("finish", 5), ("cross", 6, -2),
+    ("cross", 6, 2), ("fwd", 5, 0), ("wg", 4, 1), ("sc", 1, 2), ("cross", 6, -3), ("cross", 6, 3),
+    ("trade", 4), ("sc", 3, 0), ("sc", 2, 1), ("wg", 4, 0), ("trade", 5), ("finish", 6),
+    ("fwd", 6, 0), ("sc", 2, 2), ("wg", 5, 1), ("sc", 5, 0), ("sc", 4, 0), ("sc", 3, 1),
+    ("trade", 6), ("sc", 5, 1), ("sc", 6, 0), ("wg", 6, 1), ("sc", 4, 1), ("sc", 0, 3),
+    ("sc", 2, 3), ("sc", 3, 2), ("sc", 6, 1), ("ggout", 0), ("sc", 1, 3), ("sc", 4, 2),
+    ("sc", 5, 2), ("wg", 5, 0), ("sc", 6, 2), ("total", 2), ("wg", 6, 0), ("ggin", 0),
+    ("total", 0), ("sc", 5, 3), ("sc", 3, 3), ("sc", 4, 3), ("total", 1), ("total", 5),
+    ("sc", 6, 3), ("total", 6), ("total", 4), ("total", 3),
 ]
 
 
@@ -110,21 +119,23 @@
             steps += [("relay", k, -d), ("relay", k, d)]
         steps += [("cross", k, d) for d in range(1 - depth, depth)]
         steps += [("finish", k), ("fwd", k, 0), ("fwd", k, 1), ("wg", k, 0), ("wg", k, 1)]
-        steps += [("sc", k, p) for p in range(depth)] + [("total", k)]
+        steps += [("trade", k)] + [("sc", k, p) for p in range(depth)] + [("total", k)]
     return steps + [("ggout", 0), ("ggin", 0)]
 
 
 def fused_kernel(
     depth, order, home_cap, rep_cap,
     x_hbm, dy_hbm, gates_hbm, ids_hbm, table_hbm, wg_hbm, wu_hbm, wd_hbm,
+    out_hbm, ggo_hbm, dwg_hbm, dwu_hbm, dwd_hbm,
     out_ref, ggo_ref, dwg_ref, dwu_ref, dwd_ref,
-    buf, gbuf, gcol, ggcol, ggs, ggr, w1, wd, dadb, hgb, acc1, acc2, dx, rc, rzu, rzd, ysend, ry,
+    buf, gbuf, gcol, ggcol, ggs, ggr, w1, wd, dadb, hgb, acc1, acc2, dx, rc, rzu, rzd, ysend, ry, xsend, xr,
     gates_ref, ids_ref, table_ref,
     local_sems, send_sems, recv_sems, pair_sems, gate_sem, gg_sem, twin_sems, up_sems, down_sems,
-    y_sems,
+    y_sems, x_sems, gate_sems,
 ):
     f32, bf16 = jnp.float32, jnp.bfloat16
     devices = 4 * depth
+    early, wide = PAIR_FIRST, BOTH_COLUMNS
     me, z, y, c, last = place(depth)
     tok, width = x_hbm.shape
     hidden = wd_hbm.shape[0]
@@ -143,9 +154,13 @@
     plan_copies = [
         local(gates_hbm, gates_ref, 5), local(ids_hbm, ids_ref, 6), local(table_hbm, table_ref, 7),
     ]
+    results = [
+        local(out_ref, out_hbm, 8), local(ggo_ref, ggo_hbm, 9), local(dwg_ref, dwg_hbm, 10),
+        local(dwu_ref, dwu_hbm, 11), local(dwd_ref, dwd_hbm, 12),
+    ]
     for copy in own_copies + plan_copies + weight_copies:
         copy.start()
-    greet(me, devices)
+    greet(z, y, c, last)
     for copy in own_copies:
         copy.wait()
 
@@ -160,15 +175,23 @@
     def rows_of(k):
         return pl.ds(*chunks[k])
 
-    OWN, PASS, PAIR, CHAIN, HOME, GATE, BACK = range(7)
+    OWN, PASS, WIDE, PAIR, CHAIN, THIN, TRADE, HOME, GATE, BACK, FLAT = range(11)
 
     def push(group, cond, b, k, peer):
         block = lambda: buf.at[b(), :, rows_of(k)]
         sem = (lambda: pair_sems.at[k]) if peer is twin else (lambda: recv_sems.at[k, b()])
         out.send(group, cond, remote(block, block, sem, peer))
+        if k == 0 and group != OWN:
+            push_gates(FLAT, cond, b, peer)
+
+    def push_gates(group, cond, b, peer):
+        sem = (lambda: gate_sem) if peer is twin else (lambda: gate_sems.at[b()])
+        out.send(group, cond, remote(lambda: gbuf.at[b()], lambda: gbuf.at[b()], sem, peer))
 
     def arrived(k, b):
         landed(buf.at[b, :, rows_of(k)], recv_sems.at[k, b])
+        if k == 0:
+            landed(gbuf.at[b], gate_sems.at[b])
 
     def own(k):
         mine = lambda: me
@@ -182,19 +205,27 @@
         more, onward = (can_up, up) if off < 0 else (can_down, down)
         b = lambda: index_of(z + off, y, c)
         pl.when(cond)(lambda: arrived(k, b()))
+        group = WIDE if wide[k] else PASS
         if abs(off) < depth - 1:
-            push(PASS, cond & more, b, k, onward)
-        push(PASS, cond, b, k, over)
-        push(PASS, cond, b, k, twin)
+            push(group, cond & more, b, k, onward)
+        if not wide[k]:
+            push(group, cond, b, k, over)
+        push(group, cond, b, k, twin)
 
     def cross(k, off):
         b = lambda: index_of(z + off, 1 - y, c)
         cond = None if off == 0 else z + off >= 0 if off < 0 else z + off <= last
+        group = WIDE if wide[k] else PASS
         if cond is None:
             arrived(k, b())
         else:
             pl.when(cond)(lambda: arrived(k, b()))
-        push(PASS, cond, b, k, twin)
+        if wide[k] and abs(off) < depth - 1:
+            if off <= 0:
+                push(group, can_up if cond is None else cond & can_up, b, k, up)
+            if off >= 0:
+                push(group, can_down if cond is None else cond & can_down, b, k, down)
+        push(group, cond, b, k, twin)
 
     def finish(k):
         landed(buf.at[pl.ds(0, devices // 2), :, rows_of(k)], pair_sems.at[k])
@@ -221,17 +252,11 @@
         copy_index = turn - copies * jnp.floor((turn + 0.5) / copies)
         limit = jnp.where(copy_index < 0.5, float(home_cap), float(rep_cap))
         gbuf[me] = jnp.where((named > 0.5) & (position < limit), dense, 0.0).astype(bf16)
-        for peer in range(devices):
-            out.send(
-                GATE, peer != me,
-                remote(
-                    lambda: gbuf.at[me], lambda: gbuf.at[me], lambda: gate_sem,
-                    lambda peer=peer: peer,
-                ),
-            )
+        for cond, peer in ((None, over), (can_up, up), (can_down, down), (None, twin)):
+            push_gates(GATE, cond, lambda: me, peer)
 
     def take_gates():
-        landed(gbuf.at[pl.ds(0, devices - 1)], gate_sem)
+        landed(gbuf.at[pl.ds(0, devices // 2)], gate_sem)
         flat = gbuf[...].reshape(devices * devices, tok)
         r = lax.broadcasted_iota(jnp.int32, (devices * devices, lanes), 0)
         l = lax.broadcasted_iota(jnp.int32, (devices * devices, lanes), 1)
@@ -326,6 +351,9 @@
     def weights(k, which):
         for j in range(width // tile):
             weight_tile(k, j, which)
+        if k == len(chunks) - 1:
+            for copy in (results[2:4], results[4:])[which]:
+                copy.start()
 
     def part_sum(zz, yy, rows, extra):
         total = dx[zz, yy, c, rows, :].astype(f32) + rc[zz, yy, rows, :].astype(f32)
@@ -333,32 +361,58 @@
             total = total + ref[zz, yy, rows, :].astype(f32)
         return total
 
+    def trade(k):
+        if not early[k]:
+            return
+        twin_sums(k)
+        rows = rows_of(k)
+        for i in range(depth):
+            zz = jnp.where(2 * z < depth, last - i, i)
+            xsend[zz, rows, :] = part_sum(zz, 1 - y, rows, ()).astype(bf16)
+            out.send(
+                TRADE, None,
+                remote(
+                    lambda zz=zz: xsend.at[zz, rows, :], lambda zz=zz: xr.at[zz, rows, :],
+                    lambda zz=zz: x_sems.at[k, zz], over,
+                ),
+            )
+
+    def traded(k, zz):
+        landed(xr.at[zz, rows_of(k), :], x_sems.at[k, zz])
+        return part_sum(zz, y, rows_of(k), ()) + xr[zz, rows_of(k), :].astype(f32)
+
     def chain(k, p):
         rows = rows_of(k)
-        for way, there, zz_of, ref, sems, has, peer in (
-            (0, z <= p, lambda: z + last - p, rzu, up_sems, z > 0, up),
-            (1, last - z <= p, lambda: z + p - last, rzd, down_sems, z < last, down),
+        for there, zz, ref, sems, has, peer in (
+            (z <= p, z + last - p, rzu, up_sems, z > 0, up),
+            (last - z <= p, z + p - last, rzd, down_sems, z < last, down),
         ):
+            piece = ref.at[zz, 0, rows, :] if early[k] else ref.at[zz, :, rows, :]
 
             def step():
-                zz = zz_of()
-                pl.when(has)(lambda: landed(ref.at[zz, :, rows, :], sems.at[k, zz]))
-                for yy in range(2):
-                    ref[zz, yy, rows, :] = part_sum(zz, yy, rows, (ref,)).astype(bf16)
+                pl.when(has)(lambda: landed(piece, sems.at[k, zz]))
+                if early[k]:
+                    held = ref[zz, 0, rows, :].astype(f32)
+                    ref[zz, 0, rows, :] = (traded(k, zz) + held).astype(bf16)
+                else:
+                    for yy in range(2):
+                        ref[zz, yy, rows, :] = part_sum(zz, yy, rows, (ref,)).astype(bf16)
 
             pl.when(there)(step)
             out.send(
-                CHAIN, there,
-                remote(
-                    lambda: ref.at[zz_of(), :, rows, :], lambda: ref.at[zz_of(), :, rows, :],
-                    lambda: sems.at[k, zz_of()], peer,
-                ),
+                THIN if early[k] else CHAIN, there,
+                remote(lambda: piece, lambda: piece, lambda: sems.at[k, zz], peer),
             )
 
     def home(k):
         rows = rows_of(k)
-        pl.when(z > 0)(lambda: landed(rzu.at[z, :, rows, :], up_sems.at[k, z]))
-        pl.when(z < last)(lambda: landed(rzd.at[z, :, rows, :], down_sems.at[k, z]))
+        way = 0 if early[k] else slice(None)
+        pl.when(z > 0)(lambda: landed(rzu.at[z, way, rows, :], up_sems.at[k, z]))
+        pl.when(z < last)(lambda: landed(rzd.at[z, way, rows, :], down_sems.at[k, z]))
+        if early[k]:
+            held = rzu[z, 0, rows, :].astype(f32) + rzd[z, 0, rows, :].astype(f32)
+            out_ref[rows, :] = (traded(k, z) + held).astype(bf16)
+            return
         ysend[rows, :] = part_sum(z, 1 - y, rows, (rzu, rzd)).astype(bf16)
         out.send(
             HOME, None,
@@ -368,15 +422,17 @@
         )
 
     def total(k):
+        if early[k]:
+            return
         rows = rows_of(k)
         mine = part_sum(z, y, rows, (rzu, rzd))
         landed(ry.at[rows, :], y_sems.at[k])
         out_ref[rows, :] = (mine + ry[rows, :].astype(f32)).astype(bf16)
 
     def scatter_point(k, p):
-        if p == 0:
+        if p == 0 and not early[k]:
             twin_sums(k)
-        if p < last:
+        if p < depth - 1:
             chain(k, p)
         else:
             home(k)
@@ -402,6 +458,7 @@
             hot = ids_ref[k : k + 1] == expert
             picked = jnp.sum(jnp.where(hot, held, 0.0), axis=0, keepdims=True)
             ggo_ref[k : k + 1] = picked.astype(bf16)
+        results[1].start()
 
     def gates_out(k):
         for copy in plan_copies:
@@ -425,29 +482,48 @@
 
     steps = dict(
         own=own, gates=gates_out, relay=relay, cross=cross, finish=ready, fwd=forward,
-        wg=weights, sc=scatter_point, total=total, ggout=lambda k: send_gate_grads(),
+        wg=weights, trade=trade, sc=scatter_point, total=total, ggout=lambda k: send_gate_grads(),
         ggin=lambda k: take_gate_grads(),
     )
     for name, *rest in order:
         steps[name](*rest)
 
+    results[0].start()
+
+    def rows_in(flags, want):
+        return sum(size for (_, size), flag in zip(chunks, flags) if flag == want)
+
     def sent_blocks(zz):
-        ends = (zz < last) + (zz > 0)
-        passed = depth
+        ends = (zz < depth - 1) + (zz > 0)
+        passed, widened = depth, 1 + ends
         for off in range(1, depth):
-            passed += (zz >= off) * (2 + (zz < last and off < last))
-            passed += (zz + off <= last) * (2 + (zz > 0 and off < last))
+            mid = off < depth - 1
+            below, above = zz >= off, zz + off < depth
+            passed += below * (2 + (zz < depth - 1 and mid)) + above * (2 + (zz > 0 and mid))
+            widened += 2 * below * (1 + (zz < depth - 1 and mid))
+            widened += 2 * above * (1 + (zz > 0 and mid))
         out.sent(OWN, buf.at[pl.ds(0, 2 + ends)])
-        out.sent(PASS, buf.at[pl.ds(0, passed)])
+        out.sent(GATE, gbuf.at[pl.ds(0, 2 + ends)])
+        out.sent(FLAT, gbuf.at[pl.ds(0, widened if wide[0] else passed)])
+        for group, count, want in ((PASS, passed, False), (WIDE, widened, True)):
+            if rows_in(wide, want):
+                out.sent(group, buf.at[pl.ds(0, count), :, pl.ds(0, rows_in(wide, want))])
 
     for zz in range(depth):
         pl.when(z == zz)(lambda: sent_blocks(zz))
     out.sent(PAIR, rc)
-    if depth > 1:
-        out.sent(CHAIN, rzu.at[pl.ds(0, depth - 1)])
-    out.sent(HOME, ysend)
-    out.sent(GATE, gbuf.at[pl.ds(0, devices - 1)])
+    late, soon = rows_in(early, False), rows_in(early, True)
+    if late:
+        out.sent(HOME, ysend.at[pl.ds(0, late)])
+    if soon:
+        out.sent(TRADE, xsend.at[:, pl.ds(0, soon)])
+    if depth > 1 and late:
+        out.sent(CHAIN, rzu.at[pl.ds(0, depth - 1), :, pl.ds(0, late)])
+    if depth > 1 and soon:
+        out.sent(THIN, rzu.at[pl.ds(0, depth - 1), 0, pl.ds(0, soon)])
     out.sent(BACK, ggs.at[pl.ds(0, devices - 1)])
+    for copy in results:
+        copy.wait()
 
 
 def fused_grads(x, dy, gates, ids, table, gate_w, up_w, down_w, devices, home_cap, rep_cap):
@@ -458,7 +534,6 @@
     n = len(row_chunks(tok))
     most = max(size for _, size in row_chunks(tok))
     vmem, dma = pltpu.VMEM, pltpu.SemaphoreType.DMA
-    whole = pl.BlockSpec(memory_space=pltpu.VMEM)
     hbm = pl.BlockSpec(memory_space=pltpu.HBM)
     shape = jax.ShapeDtypeStruct
     outs = pl.pallas_call(
@@ -468,8 +543,10 @@
             shape(up_w.shape, bf16), shape(down_w.shape, bf16),
         ],
         in_specs=[hbm] * 8,
-        out_specs=[whole] * 5,
+        out_specs=[hbm] * 5,
         scratch_shapes=[
+            vmem((tok, width), bf16), vmem(gates.shape, bf16), vmem(gate_w.shape, bf16),
+            vmem(up_w.shape, bf16), vmem(down_w.shape, bf16),
             vmem((devices, 2, tok, width), bf16), vmem((devices, devices, tok), bf16),
             vmem((tok, 128), f32), vmem((tok, 128), f32),
             vmem((devices, 1, tok), f32), vmem((devices, 1, tok), f32),
@@ -479,10 +556,11 @@
             vmem((depth, 2, 2, tok, width), bf16), vmem((depth, 2, tok, width), bf16),
             vmem((depth, 2, tok, width), bf16), vmem((depth, 2, tok, width), bf16),
             vmem((tok, width), bf16), vmem((tok, width), bf16),
+            vmem((depth, tok, width), bf16), vmem((depth, tok, width), bf16),
             vmem(gates.shape, bf16), vmem(ids.shape, ids.dtype),
             pltpu.SMEM(table.shape, table.dtype),
-            dma((8,)), dma((7,)), dma((n, devices)), dma((n,)), dma, dma,
-            dma((n, 2)), dma((n, depth)), dma((n, depth)), dma((n,)),
+            dma((13,)), dma((12,)), dma((n, devices)), dma((n,)), dma, dma,
+            dma((n, 2)), dma((n, depth)), dma((n, depth)), dma((n,)), dma((n, depth)), dma((devices,)),
         ],
         compiler_params=pltpu.CompilerParams(
             collective_id=0, has_side_effects=True, vmem_limit_bytes=VMEM_GRANT
@@ -491,25 +569,41 @@
     return store_all(outs)
 
 
-def store_kernel(n, *refs):
-    sems = refs[2 * n]
-    copies = [
-        pltpu.make_async_copy(refs[i], refs[n + i], sems.at[i]) for i in range(n)
-    ]
-    for copy in copies:
+def store_kernel(n, cuts, *refs):
+    src, dst, held, (load_sems, store_sems) = refs[:n], refs[n : 2 * n], refs[2 * n : -2], refs[-2:]
+    loads, stores = [], []
+    for i in range(n):
+        step = src[i].shape[0] // cuts[i]
+        for j in range(cuts[i]):
+            rows = pl.ds(j * step, step)
+            m = len(loads)
+            loads.append(
+                pltpu.make_async_copy(src[i].at[rows], held[i].at[rows], load_sems.at[m])
+            )
+            stores.append(
+                pltpu.make_async_copy(held[i].at[rows], dst[i].at[rows], store_sems.at[m])
+            )
+    for copy in loads:
         copy.start()
-    for copy in copies:
+    for load, store in zip(loads, stores):
+        load.wait()
+        store.start()
+    for copy in stores:
         copy.wait()
 
 
 def store_all(arrays):
     n = len(arrays)
+    cuts = [2 if v.shape[0] >= 256 and v.shape[0] % 64 == 0 else 1 for v in arrays]
+    hbm = pl.BlockSpec(memory_space=pltpu.HBM)
     return pl.pallas_call(
-        lambda *refs: store_kernel(n, *refs),
+        lambda *refs: store_kernel(n, cuts, *refs),
         out_shape=[jax.ShapeDtypeStruct(v.shape, v.dtype) for v in arrays],
-        in_specs=[pl.BlockSpec(memory_space=pltpu.VMEM)] * n,
-        out_specs=[pl.BlockSpec(memory_space=pltpu.HBM)] * n,
-        scratch_shapes=[pltpu.SemaphoreType.DMA((n,))],
+        in_specs=[hbm] * n,
+        out_specs=[hbm] * n,
+        scratch_shapes=[pltpu.VMEM(v.shape, v.dtype) for v in arrays]
+        + [pltpu.SemaphoreType.DMA((sum(cuts),))] * 2,
+        compiler_params=pltpu.CompilerParams(vmem_limit_bytes=VMEM_GRANT),
     )(*arrays)
 
 

time: 88.9 us -> 75.3 us (0.85)
  Pallas kernels: 88 us -> 74.4 us
    pallas_call x1, Pallas kernels: 84.7 us -> 71.8 us  [fused_grads(): pl.pallas_call(lambda *refs: fused_kernel(depth, step_order(depth, n), ho...]
where the time goes in v2:
time: 75.3 us; the launch traced here: 75.2 us
  Pallas kernels  74.4 us (99%)
  between operations  0.8 us (1%)
    pallas_call x1, Pallas kernels, fused_grads(): pl.pallas_call(lambda *refs: fused_kernel(depth, step_order(depth, n), ho...  71.8 us
    pallas_call x1, Pallas kernels, store_all(): pl.pallas_call(lambda *refs: store_kernel(n, cuts, *refs), out_shape=[jax...  2.61 us

profile of v2, /device:TPU:0, one launch (start us, length us, event | category | flops | bytes accessed | tf_op | source)
XLA Modules:
  0.0 75.2 jit_solution(8872648269439173072)
XLA Ops:
  0.6 71.8 %shard_map.119 = (bf16[128,1024]{1,0:T(8,128)(2,1)}, bf16[8,128]{1,0:T(8,128)(2,1)}, bf16[1024,384]{1,0:T(8,128)(2,1)}, bf16[1024,384]{1,0:T(8,128)(2,1)}, bf16[384,1024]{1,0:T(8,128)(2,1)}) custom-call(bf16[128,1024]{1,0:T(8,128)(2,1)} %refs_0_.1, bf16[128,1024]{1,0:T(8,128)(2,1)} %refs_1_.1, bf16[8,128]{1,0:T(8,128)(2,1)} %bitcast.13, s32[8,128]{1,0:T(8,128)} %bitcast.12, ...), custom_call_target="tpu_custom_call" | custom-call | tf_op jit(solution)/shard_map/pallas_call | solution.py:539
  72.4 2.6 %shard_map.120 = (bf16[128,1024]{1,0:T(8,128)(2,1)}, bf16[8,128]{1,0:T(8,128)(2,1)}, bf16[1024,384]{1,0:T(8,128)(2,1)}, bf16[1024,384]{1,0:T(8,128)(2,1)}, bf16[384,1024]{1,0:T(8,128)(2,1)}) custom-call(bf16[128,1024]{1,0:T(8,128)(2,1)} %get-tuple-element.15.refs_0_, bf16[8,128]{1,0:T(8,128)(2,1)} %get-tuple-element.16.refs_1_, ...), custom_call_target="tpu_custom_call" | custom-call | tf_op jit(solution)/shard_map/pallas_call | solution.py:599

commit v3 on v2

--- a/solution.py
+++ b/solution.py
@@ -64,42 +64,38 @@
 
 
 TUNED_DEPTH = 4
-TUNED_SHARES = (32, 16, 16, 16, 16, 16, 16)
-PAIR_FIRST = (False, False, False, True, True, True, True)
-BOTH_COLUMNS = (False, False, False, True, False, False, False)
+TUNED_SHARES = (16, 32, 32, 16, 16, 16)
+PAIR_FIRST = (False, False, True, True, True, True)
+BOTH_COLUMNS = (False, False, False, True, False, True)
 TUNED = [
-    ("own", 0), ("own", 1), ("gates", 0), ("own", 2), ("relay", 0, 1), ("relay", 0, -1),
-    ("own", 3), ("relay", 1, 1), ("relay", 0, 2), ("relay", 1, -1), ("relay", 1, 2),
-    ("relay", 0, -2), ("relay", 1, -2), ("relay", 0, -3), ("relay", 0, 3), ("relay", 2, -1),
-    ("relay", 2, 1), ("cross", 1, 1), ("cross", 0, 0), ("cross", 1, 0), ("relay", 1, -3),
-    ("relay", 1, 3), ("cross", 2, 0), ("cross", 3, 0), ("cross", 0, 1), ("relay", 2, 2),
-    ("cross", 0, 2), ("cross", 0, -1), ("relay", 2, -2), ("relay", 3, -1), ("own", 4),
-    ("cross", 0, -2), ("relay", 3, 1), ("cross", 0, 3), ("cross", 1, -1), ("relay", 2, 3),
-    ("cross", 0, -3), ("relay", 2, -3), ("own", 5), ("cross", 3, 1), ("cross", 3, -1),
-    ("cross", 1, -2), ("own", 6), ("finish", 0), ("fwd", 0, 0), ("fwd", 0, 1), ("trade", 0),
-    ("cross", 1, 2), ("cross", 1, 3), ("cross", 2, -1), ("relay", 4, 1), ("relay", 5, 1),
-    ("relay", 4, -1), ("wg", 0, 1), ("cross", 1, -3), ("cross", 2, 1), ("wg", 0, 0),
-    ("cross", 4, 0), ("relay", 3, -2), ("relay", 5, -1), ("cross", 2, -2), ("cross", 2, 2),
-    ("cross", 3, 2), ("sc", 0, 0), ("finish", 1), ("cross", 2, 3), ("cross", 2, -3),
-    ("fwd", 1, 0), ("cross", 3, -2), ("relay", 3, 2), ("finish", 2), ("relay", 4, 2),
-    ("relay", 4, -2), ("fwd", 2, 0), ("wg", 1, 0), ("relay", 5, 2), ("trade", 1), ("cross", 5, 0),
-    ("cross", 6, 0), ("relay", 3, -3), ("relay", 5, -2), ("cross", 3, 3), ("relay", 6, 1),
-    ("cross", 4, 1), ("wg", 1, 1), ("relay", 6, -1), ("sc", 0, 1), ("cross", 3, -3), ("sc", 1, 0),
-    ("relay", 3, 3), ("wg", 2, 1), ("trade", 2), ("wg", 2, 0), ("relay", 4, 3), ("cross", 4, -1),
-    ("relay", 4, -3), ("finish", 3), ("fwd", 3, 0), ("relay", 5, 3), ("relay", 5, -3),
-    ("wg", 3, 1), ("sc", 2, 0), ("relay", 6, -2), ("relay", 6, 2), ("sc", 0, 2), ("cross", 4, -3),
-    ("cross", 4, 3), ("cross", 4, -2), ("cross", 5, -1), ("sc", 1, 1), ("cross", 4, 2),
-    ("cross", 5, 2), ("wg", 3, 0), ("cross", 5, 1), ("cross", 6, 1), ("cross", 5, -2),
-    ("cross", 6, -1), ("relay", 6, 3), ("relay", 6, -3), ("trade", 3), ("cross", 5, 3),
-    ("cross", 5, -3), ("finish", 4), ("fwd", 4, 0), ("finish", 5), ("cross", 6, -2),
-    ("cross", 6, 2), ("fwd", 5, 0), ("wg", 4, 1), ("sc", 1, 2), ("cross", 6, -3), ("cross", 6, 3),
-    ("trade", 4), ("sc", 3, 0), ("sc", 2, 1), ("wg", 4, 0), ("trade", 5), ("finish", 6),
-    ("fwd", 6, 0), ("sc", 2, 2), ("wg", 5, 1), ("sc", 5, 0), ("sc", 4, 0), ("sc", 3, 1),
-    ("trade", 6), ("sc", 5, 1), ("sc", 6, 0), ("wg", 6, 1), ("sc", 4, 1), ("sc", 0, 3),
-    ("sc", 2, 3), ("sc", 3, 2), ("sc", 6, 1), ("ggout", 0), ("sc", 1, 3), ("sc", 4, 2),
-    ("sc", 5, 2), ("wg", 5, 0), ("sc", 6, 2), ("total", 2), ("wg", 6, 0), ("ggin", 0),
-    ("total", 0), ("sc", 5, 3), ("sc", 3, 3), ("sc", 4, 3), ("total", 1), ("total", 5),
-    ("sc", 6, 3), ("total", 6), ("total", 4), ("total", 3),
+    ("own", 0), ("gates", 0), ("own", 1), ("relay", 0, 1), ("relay", 0, -1), ("relay", 1, 1),
+    ("relay", 0, 2), ("relay", 1, -1), ("cross", 0, 0), ("relay", 0, -2), ("cross", 1, 0),
+    ("own", 2), ("cross", 1, 1), ("relay", 0, 3), ("relay", 0, -3), ("relay", 1, 2),
+    ("cross", 0, 2), ("cross", 0, 1), ("relay", 1, -2), ("cross", 0, 3), ("cross", 0, -1),
+    ("own", 3), ("relay", 1, 3), ("relay", 2, 1), ("cross", 0, -2), ("cross", 0, -3),
+    ("relay", 1, -3), ("finish", 0), ("relay", 2, -1), ("fwd", 0, 0), ("relay", 2, -2),
+    ("relay", 3, -1), ("relay", 2, 2), ("trade", 0), ("wg", 0, 0), ("cross", 1, 2),
+    ("cross", 1, -1), ("cross", 1, -2), ("cross", 1, 3), ("relay", 2, 3), ("cross", 1, -3),
+    ("cross", 3, 0), ("relay", 2, -3), ("own", 4), ("cross", 2, 0), ("relay", 3, 1), ("sc", 0, 0),
+    ("finish", 1), ("fwd", 1, 0), ("own", 5), ("fwd", 1, 1), ("cross", 3, -1), ("wg", 0, 1),
+    ("cross", 2, -1), ("relay", 4, 1), ("cross", 3, 1), ("relay", 4, -1), ("cross", 2, 1),
+    ("wg", 1, 0), ("sc", 0, 1), ("cross", 2, 2), ("relay", 3, 2), ("cross", 2, -2),
+    ("cross", 2, -3), ("cross", 2, 3), ("relay", 4, 2), ("cross", 3, -2), ("trade", 1),
+    ("sc", 1, 0), ("wg", 1, 1), ("relay", 4, -2), ("relay", 3, -2), ("cross", 3, 2),
+    ("finish", 2), ("fwd", 2, 0), ("cross", 5, 0), ("fwd", 2, 1), ("relay", 4, -3),
+    ("relay", 4, 3), ("relay", 5, 1), ("relay", 5, -1), ("wg", 2, 0), ("cross", 3, 3),
+    ("relay", 3, -3), ("cross", 3, -3), ("relay", 3, 3), ("wg", 2, 1), ("cross", 5, 1),
+    ("cross", 5, -1), ("trade", 2), ("cross", 4, -1), ("cross", 4, 0), ("cross", 4, 1),
+    ("sc", 1, 1), ("cross", 4, -3), ("cross", 4, -2), ("finish", 3), ("cross", 4, 2),
+    ("cross", 4, 3), ("relay", 5, 2), ("relay", 5, -2), ("fwd", 3, 0), ("cross", 5, 2),
+    ("finish", 4), ("cross", 5, -2), ("sc", 0, 2), ("fwd", 4, 0), ("sc", 2, 0), ("relay", 5, -3),
+    ("relay", 5, 3), ("trade", 3), ("wg", 3, 1), ("cross", 5, 3), ("cross", 5, -3), ("sc", 1, 2),
+    ("wg", 3, 0), ("trade", 4), ("finish", 5), ("fwd", 5, 0), ("sc", 2, 1), ("ggout", 0),
+    ("sc", 3, 0), ("sc", 4, 0), ("trade", 5), ("sc", 2, 2), ("wg", 4, 1), ("sc", 5, 0),
+    ("sc", 4, 1), ("sc", 3, 1), ("sc", 0, 3), ("wg", 5, 1), ("sc", 1, 3), ("wg", 4, 0),
+    ("sc", 5, 1), ("sc", 4, 2), ("sc", 3, 2), ("total", 0), ("total", 1), ("sc", 5, 2),
+    ("ggin", 0), ("sc", 4, 3), ("sc", 3, 3), ("total", 3), ("sc", 2, 3), ("wg", 5, 0),
+    ("total", 2), ("sc", 5, 3), ("total", 5), ("total", 4),
 ]
 
 
@@ -107,6 +103,11 @@
     whole = sum(TUNED_SHARES)
     sizes = [tok * share // whole for share in TUNED_SHARES]
     return [(sum(sizes[:k]), size) for k, size in enumerate(sizes)]
+
+
+def unit_counts(tok, devices):
+    whole = devices % 8 != 0
+    return [1 if whole or size * devices <= 256 else 2 for _, size in row_chunks(tok)]
 
 
 def step_order(depth, n):
@@ -130,12 +131,13 @@
     out_ref, ggo_ref, dwg_ref, dwu_ref, dwd_ref,
     buf, gbuf, gcol, ggcol, ggs, ggr, w1, wd, dadb, hgb, acc1, acc2, dx, rc, rzu, rzd, ysend, ry, xsend, xr,
     gates_ref, ids_ref, table_ref,
-    local_sems, send_sems, recv_sems, pair_sems, gate_sem, gg_sem, twin_sems, up_sems, down_sems,
+    local_sems, send_sems, recv_sems, pair_sems, gate_sem, gg_sem, twin_sems, chain_sems,
     y_sems, x_sems, gate_sems,
 ):
     f32, bf16 = jnp.float32, jnp.bfloat16
     devices = 4 * depth
     early, wide = PAIR_FIRST, BOTH_COLUMNS
+    counts = unit_counts(x_hbm.shape[0], devices)
     me, z, y, c, last = place(depth)
     tok, width = x_hbm.shape
     hidden = wd_hbm.shape[0]
@@ -145,24 +147,23 @@
     def local(src, dst, i):
         return pltpu.make_async_copy(src, dst, local_sems.at[i])
 
-    own_copies = [local(x_hbm, buf.at[me, 0], 0), local(dy_hbm, buf.at[me, 1], 1)]
+    own_copies = [local(x_hbm, buf.at[me, 0], 0), local(dy_hbm, buf.at[me, 1], 0)]
     weight_copies = [
-        local(wg_hbm, w1.at[:, pl.ds(0, hidden)], 2),
-        local(wu_hbm, w1.at[:, pl.ds(hidden, hidden)], 3),
-        local(wd_hbm, wd, 4),
+        local(wg_hbm, w1.at[:, pl.ds(0, hidden)], 1),
+        local(wu_hbm, w1.at[:, pl.ds(hidden, hidden)], 1),
+        local(wd_hbm, wd, 2),
     ]
     plan_copies = [
-        local(gates_hbm, gates_ref, 5), local(ids_hbm, ids_ref, 6), local(table_hbm, table_ref, 7),
+        local(gates_hbm, gates_ref, 3), local(ids_hbm, ids_ref, 4), local(table_hbm, table_ref, 5),
     ]
     results = [
-        local(out_ref, out_hbm, 8), local(ggo_ref, ggo_hbm, 9), local(dwg_ref, dwg_hbm, 10),
-        local(dwu_ref, dwu_hbm, 11), local(dwd_ref, dwd_hbm, 12),
+        local(out_ref, out_hbm, 6), local(ggo_ref, ggo_hbm, 7), local(dwg_ref, dwg_hbm, 8),
+        local(dwu_ref, dwu_hbm, 9), local(dwd_ref, dwd_hbm, 10),
     ]
     for copy in own_copies + plan_copies + weight_copies:
         copy.start()
     greet(z, y, c, last)
-    for copy in own_copies:
-        copy.wait()
+    landed(buf.at[me], local_sems.at[0])
 
     out = Sender(send_sems)
     up = lambda: index_of(z + 1, y, c)
@@ -179,19 +180,19 @@
 
     def push(group, cond, b, k, peer):
         block = lambda: buf.at[b(), :, rows_of(k)]
-        sem = (lambda: pair_sems.at[k]) if peer is twin else (lambda: recv_sems.at[k, b()])
+        sem = (lambda: pair_sems.at[k]) if peer is twin else (lambda: recv_sems.at[k, b() // 2])
         out.send(group, cond, remote(block, block, sem, peer))
         if k == 0 and group != OWN:
             push_gates(FLAT, cond, b, peer)
 
     def push_gates(group, cond, b, peer):
-        sem = (lambda: gate_sem) if peer is twin else (lambda: gate_sems.at[b()])
+        sem = (lambda: gate_sem) if peer is twin else (lambda: gate_sems.at[b() // 2])
         out.send(group, cond, remote(lambda: gbuf.at[b()], lambda: gbuf.at[b()], sem, peer))
 
     def arrived(k, b):
-        landed(buf.at[b, :, rows_of(k)], recv_sems.at[k, b])
+        landed(buf.at[b, :, rows_of(k)], recv_sems.at[k, b // 2])
         if k == 0:
-            landed(gbuf.at[b], gate_sems.at[b])
+            landed(gbuf.at[b], gate_sems.at[b // 2])
 
     def own(k):
         mine = lambda: me
@@ -265,7 +266,7 @@
         ggcol[...] = jnp.zeros_like(ggcol)
 
     def units(k):
-        if chunks[k][1] * devices <= 256 or depth % 2:
+        if counts[k] == 1:
             return [(0, depth)]
         first = jnp.where(z < half, half, 0)
         return [(first, half), (half - first, half)]
@@ -313,11 +314,11 @@
         ggcol[rows, :] = held
         src = lambda: dx.at[pl.ds(p0, planes), :, 1 - c, rows, :]
         dst = lambda: rc.at[pl.ds(p0, planes), :, rows, :]
-        out.send(PAIR, None, remote(src, dst, lambda: twin_sems.at[k, u], twin))
+        out.send(PAIR, None, remote(src, dst, lambda: twin_sems.at[sum(counts[:k]) + u], twin))
 
     def twin_sums(k):
         for u, (p0, planes) in enumerate(units(k)):
-            landed(rc.at[pl.ds(p0, planes), :, rows_of(k), :], twin_sems.at[k, u])
+            landed(rc.at[pl.ds(p0, planes), :, rows_of(k), :], twin_sems.at[sum(counts[:k]) + u])
 
     tile = 256 if width % 256 == 0 else 128
 
@@ -373,24 +374,24 @@
                 TRADE, None,
                 remote(
                     lambda zz=zz: xsend.at[zz, rows, :], lambda zz=zz: xr.at[zz, rows, :],
-                    lambda zz=zz: x_sems.at[k, zz], over,
+                    lambda zz=zz: x_sems.at[sum(early[:k]), zz], over,
                 ),
             )
 
     def traded(k, zz):
-        landed(xr.at[zz, rows_of(k), :], x_sems.at[k, zz])
+        landed(xr.at[zz, rows_of(k), :], x_sems.at[sum(early[:k]), zz])
         return part_sum(zz, y, rows_of(k), ()) + xr[zz, rows_of(k), :].astype(f32)
 
     def chain(k, p):
         rows = rows_of(k)
-        for there, zz, ref, sems, has, peer in (
-            (z <= p, z + last - p, rzu, up_sems, z > 0, up),
-            (last - z <= p, z + p - last, rzd, down_sems, z < last, down),
+        for there, zz, ref, way, has, peer in (
+            (z <= p, z + last - p, rzu, 1, z > 0, up),
+            (last - z <= p, z + p - last, rzd, 0, z < last, down),
         ):
             piece = ref.at[zz, 0, rows, :] if early[k] else ref.at[zz, :, rows, :]
 
             def step():
-                pl.when(has)(lambda: landed(piece, sems.at[k, zz]))
+                pl.when(has)(lambda: landed(piece, chain_sems.at[k, zz + way]))
                 if early[k]:
                     held = ref[zz, 0, rows, :].astype(f32)
                     ref[zz, 0, rows, :] = (traded(k, zz) + held).astype(bf16)
@@ -401,23 +402,24 @@
             pl.when(there)(step)
             out.send(
                 THIN if early[k] else CHAIN, there,
-                remote(lambda: piece, lambda: piece, lambda: sems.at[k, zz], peer),
+                remote(lambda: piece, lambda: piece, lambda: chain_sems.at[k, zz + way], peer),
             )
 
     def home(k):
         rows = rows_of(k)
         way = 0 if early[k] else slice(None)
-        pl.when(z > 0)(lambda: landed(rzu.at[z, way, rows, :], up_sems.at[k, z]))
-        pl.when(z < last)(lambda: landed(rzd.at[z, way, rows, :], down_sems.at[k, z]))
+        pl.when(z > 0)(lambda: landed(rzu.at[z, way, rows, :], chain_sems.at[k, z + 1]))
+        pl.when(z < last)(lambda: landed(rzd.at[z, way, rows, :], chain_sems.at[k, z]))
         if early[k]:
             held = rzu[z, 0, rows, :].astype(f32) + rzd[z, 0, rows, :].astype(f32)
             out_ref[rows, :] = (traded(k, z) + held).astype(bf16)
+            local(out_ref.at[rows], out_hbm.at[rows], 6).start()
             return
         ysend[rows, :] = part_sum(z, 1 - y, rows, (rzu, rzd)).astype(bf16)
         out.send(
             HOME, None,
             remote(
-                lambda: ysend.at[rows, :], lambda: ry.at[rows, :], lambda: y_sems.at[k], over
+                lambda: ysend.at[rows, :], lambda: ry.at[rows, :], lambda: y_sems.at[k - sum(early[:k])], over
             ),
         )
 
@@ -426,8 +428,9 @@
             return
         rows = rows_of(k)
         mine = part_sum(z, y, rows, (rzu, rzd))
-        landed(ry.at[rows, :], y_sems.at[k])
+        landed(ry.at[rows, :], y_sems.at[k - sum(early[:k])])
         out_ref[rows, :] = (mine + ry[rows, :].astype(f32)).astype(bf16)
+        local(out_ref.at[rows], out_hbm.at[rows], 6).start()
 
     def scatter_point(k, p):
         if p == 0 and not early[k]:
@@ -477,8 +480,8 @@
         finish(k)
         if k == 0:
             take_gates()
-            for copy in weight_copies:
-                copy.wait()
+            landed(w1, local_sems.at[1])
+            weight_copies[2].wait()
 
     steps = dict(
         own=own, gates=gates_out, relay=relay, cross=cross, finish=ready, fwd=forward,
@@ -487,8 +490,6 @@
     )
     for name, *rest in order:
         steps[name](*rest)
-
-    results[0].start()
 
     def rows_in(flags, want):
         return sum(size for (_, size), flag in zip(chunks, flags) if flag == want)
@@ -559,8 +560,10 @@
             vmem((depth, tok, width), bf16), vmem((depth, tok, width), bf16),
             vmem(gates.shape, bf16), vmem(ids.shape, ids.dtype),
             pltpu.SMEM(table.shape, table.dtype),
-            dma((13,)), dma((12,)), dma((n, devices)), dma((n,)), dma, dma,
-            dma((n, 2)), dma((n, depth)), dma((n, depth)), dma((n,)), dma((n, depth)), dma((devices,)),
+            dma((12,)), dma((11,)), dma((n, devices // 2)), dma((n,)), dma, dma,
+            dma((sum(unit_counts(tok, devices)),)), dma((n, depth + 1)),
+            dma((max(1, n - sum(PAIR_FIRST)),)), dma((max(1, sum(PAIR_FIRST)), depth)),
+            dma((devices // 2,)),
         ],
         compiler_params=pltpu.CompilerParams(
             collective_id=0, has_side_effects=True, vmem_limit_bytes=VMEM_GRANT
@@ -594,7 +597,7 @@
 
 def store_all(arrays):
     n = len(arrays)
-    cuts = [2 if v.shape[0] >= 256 and v.shape[0] % 64 == 0 else 1 for v in arrays]
+    cuts = [4 if v.shape[0] >= 256 and v.shape[0] % 64 == 0 else 1 for v in arrays]
     hbm = pl.BlockSpec(memory_space=pltpu.HBM)
     return pl.pallas_call(
         lambda *refs: store_kernel(n, cuts, *refs),

time: 75.3 us -> 74.2 us (0.985)
  Pallas kernels: 74.4 us -> 73.2 us
    pallas_call x1, Pallas kernels: 71.8 us -> 70.5 us  [fused_grads(): pl.pallas_call(lambda *refs: fused_kernel(depth, step_order(depth, n), ho...]
where the time goes in v3:
time: 74.2 us; the launch traced here: 74 us
  Pallas kernels  73.2 us (99%)
  between operations  0.82 us (1%)
    pallas_call x1, Pallas kernels, fused_grads(): pl.pallas_call(lambda *refs: fused_kernel(depth, step_order(depth, n), ho...  70.5 us
    pallas_call x1, Pallas kernels, store_all(): pl.pallas_call(lambda *refs: store_kernel(n, cuts, *refs), out_shape=[jax...  2.7 us

profile of v3, /device:TPU:0, one launch (start us, length us, event | category | flops | bytes accessed | tf_op | source)
XLA Modules:
  0.0 74.0 jit_solution(2824042296878474928)
XLA Ops:
  0.6 70.5 %shard_map.119 = (bf16[128,1024]{1,0:T(8,128)(2,1)}, bf16[8,128]{1,0:T(8,128)(2,1)}, bf16[1024,384]{1,0:T(8,128)(2,1)}, bf16[1024,384]{1,0:T(8,128)(2,1)}, bf16[384,1024]{1,0:T(8,128)(2,1)}) custom-call(bf16[128,1024]{1,0:T(8,128)(2,1)} %refs_0_.1, bf16[128,1024]{1,0:T(8,128)(2,1)} %refs_1_.1, bf16[8,128]{1,0:T(8,128)(2,1)} %bitcast.13, s32[8,128]{1,0:T(8,128)} %bitcast.12, ...), custom_call_target="tpu_custom_call" | custom-call | tf_op jit(solution)/shard_map/pallas_call | solution.py:540
  71.1 2.7 %shard_map.120 = (bf16[128,1024]{1,0:T(8,128)(2,1)}, bf16[8,128]{1,0:T(8,128)(2,1)}, bf16[1024,384]{1,0:T(8,128)(2,1)}, bf16[1024,384]{1,0:T(8,128)(2,1)}, bf16[384,1024]{1,0:T(8,128)(2,1)}) custom-call(bf16[128,1024]{1,0:T(8,128)(2,1)} %get-tuple-element.15.refs_0_, bf16[8,128]{1,0:T(8,128)(2,1)} %get-tuple-element.16.refs_1_, ...), custom_call_target="tpu_custom_call" | custom-call | tf_op jit(solution)/shard_map/pallas_call | solution.py:602

commit v4 on v3

--- a/solution.py
+++ b/solution.py
@@ -66,36 +66,37 @@
 TUNED_DEPTH = 4
 TUNED_SHARES = (16, 32, 32, 16, 16, 16)
 PAIR_FIRST = (False, False, True, True, True, True)
-BOTH_COLUMNS = (False, False, False, True, False, True)
+STRAIGHT = (False, False, True, True, True, True)
+BOTH_COLUMNS = (False, False, False, True, True, False)
 TUNED = [
-    ("own", 0), ("gates", 0), ("own", 1), ("relay", 0, 1), ("relay", 0, -1), ("relay", 1, 1),
-    ("relay", 0, 2), ("relay", 1, -1), ("cross", 0, 0), ("relay", 0, -2), ("cross", 1, 0),
-    ("own", 2), ("cross", 1, 1), ("relay", 0, 3), ("relay", 0, -3), ("relay", 1, 2),
-    ("cross", 0, 2), ("cross", 0, 1), ("relay", 1, -2), ("cross", 0, 3), ("cross", 0, -1),
-    ("own", 3), ("relay", 1, 3), ("relay", 2, 1), ("cross", 0, -2), ("cross", 0, -3),
-    ("relay", 1, -3), ("finish", 0), ("relay", 2, -1), ("fwd", 0, 0), ("relay", 2, -2),
-    ("relay", 3, -1), ("relay", 2, 2), ("trade", 0), ("wg", 0, 0), ("cross", 1, 2),
-    ("cross", 1, -1), ("cross", 1, -2), ("cross", 1, 3), ("relay", 2, 3), ("cross", 1, -3),
-    ("cross", 3, 0), ("relay", 2, -3), ("own", 4), ("cross", 2, 0), ("relay", 3, 1), ("sc", 0, 0),
-    ("finish", 1), ("fwd", 1, 0), ("own", 5), ("fwd", 1, 1), ("cross", 3, -1), ("wg", 0, 1),
-    ("cross", 2, -1), ("relay", 4, 1), ("cross", 3, 1), ("relay", 4, -1), ("cross", 2, 1),
-    ("wg", 1, 0), ("sc", 0, 1), ("cross", 2, 2), ("relay", 3, 2), ("cross", 2, -2),
-    ("cross", 2, -3), ("cross", 2, 3), ("relay", 4, 2), ("cross", 3, -2), ("trade", 1),
-    ("sc", 1, 0), ("wg", 1, 1), ("relay", 4, -2), ("relay", 3, -2), ("cross", 3, 2),
-    ("finish", 2), ("fwd", 2, 0), ("cross", 5, 0), ("fwd", 2, 1), ("relay", 4, -3),
-    ("relay", 4, 3), ("relay", 5, 1), ("relay", 5, -1), ("wg", 2, 0), ("cross", 3, 3),
-    ("relay", 3, -3), ("cross", 3, -3), ("relay", 3, 3), ("wg", 2, 1), ("cross", 5, 1),
-    ("cross", 5, -1), ("trade", 2), ("cross", 4, -1), ("cross", 4, 0), ("cross", 4, 1),
-    ("sc", 1, 1), ("cross", 4, -3), ("cross", 4, -2), ("finish", 3), ("cross", 4, 2),
-    ("cross", 4, 3), ("relay", 5, 2), ("relay", 5, -2), ("fwd", 3, 0), ("cross", 5, 2),
-    ("finish", 4), ("cross", 5, -2), ("sc", 0, 2), ("fwd", 4, 0), ("sc", 2, 0), ("relay", 5, -3),
-    ("relay", 5, 3), ("trade", 3), ("wg", 3, 1), ("cross", 5, 3), ("cross", 5, -3), ("sc", 1, 2),
-    ("wg", 3, 0), ("trade", 4), ("finish", 5), ("fwd", 5, 0), ("sc", 2, 1), ("ggout", 0),
-    ("sc", 3, 0), ("sc", 4, 0), ("trade", 5), ("sc", 2, 2), ("wg", 4, 1), ("sc", 5, 0),
-    ("sc", 4, 1), ("sc", 3, 1), ("sc", 0, 3), ("wg", 5, 1), ("sc", 1, 3), ("wg", 4, 0),
-    ("sc", 5, 1), ("sc", 4, 2), ("sc", 3, 2), ("total", 0), ("total", 1), ("sc", 5, 2),
-    ("ggin", 0), ("sc", 4, 3), ("sc", 3, 3), ("total", 3), ("sc", 2, 3), ("wg", 5, 0),
-    ("total", 2), ("sc", 5, 3), ("total", 5), ("total", 4),
+    ("own", 0), ("gates", 0), ("own", 1), ("relay", 0, -1), ("relay", 0, 1), ("own", 3),
+    ("relay", 1, -1), ("relay", 0, -2), ("relay", 0, 2), ("cross", 0, 1), ("relay", 1, 1),
+    ("cross", 0, -1), ("relay", 0, 3), ("own", 2), ("relay", 0, -3), ("cross", 0, 0),
+    ("relay", 1, -2), ("relay", 1, 2), ("cross", 0, 2), ("cross", 0, -3), ("cross", 1, 0),
+    ("cross", 0, -2), ("cross", 0, 3), ("relay", 1, -3), ("relay", 1, 3), ("relay", 2, -1),
+    ("relay", 2, 1), ("cross", 1, 1), ("cross", 1, -1), ("finish", 0), ("fwd", 0, 0),
+    ("wg", 0, 0), ("relay", 2, -2), ("trade", 0), ("relay", 2, 2), ("cross", 3, 0),
+    ("cross", 2, 0), ("relay", 3, -1), ("wg", 0, 1), ("sc", 0, 0), ("cross", 1, -2),
+    ("cross", 1, 2), ("cross", 1, -3), ("relay", 2, -3), ("cross", 1, 3), ("relay", 2, 3),
+    ("own", 4), ("relay", 3, 1), ("own", 5), ("finish", 1), ("fwd", 1, 0), ("cross", 3, -1),
+    ("cross", 3, 1), ("fwd", 1, 1), ("cross", 2, -1), ("cross", 2, 1), ("wg", 1, 1),
+    ("relay", 5, -1), ("relay", 5, 1), ("relay", 3, 2), ("relay", 4, -1), ("sc", 0, 1),
+    ("cross", 2, 2), ("cross", 2, -2), ("trade", 1), ("cross", 2, -3), ("sc", 1, 0),
+    ("cross", 2, 3), ("wg", 1, 0), ("relay", 5, -2), ("cross", 3, -2), ("relay", 5, 2),
+    ("cross", 3, 2), ("cross", 4, 0), ("finish", 2), ("fwd", 2, 0), ("relay", 3, -2),
+    ("relay", 4, 1), ("fwd", 2, 1), ("relay", 5, 3), ("relay", 3, 3), ("relay", 5, -3),
+    ("sc", 0, 2), ("wg", 2, 1), ("cross", 3, 3), ("cross", 3, -3), ("wg", 2, 0), ("cross", 4, 1),
+    ("trade", 2), ("cross", 4, -1), ("cross", 5, 2), ("cross", 5, 1), ("relay", 3, -3),
+    ("relay", 4, 2), ("relay", 4, -2), ("sc", 1, 1), ("finish", 3), ("cross", 5, -1),
+    ("fwd", 3, 0), ("wg", 3, 0), ("cross", 5, 0), ("relay", 4, -3), ("cross", 5, 3),
+    ("cross", 4, -2), ("cross", 4, 2), ("sc", 0, 3), ("cross", 5, -2), ("cross", 5, -3),
+    ("sc", 2, 0), ("relay", 4, 3), ("cross", 4, 3), ("sc", 1, 2), ("sc", 2, 1), ("cross", 4, -3),
+    ("trade", 3), ("finish", 4), ("fwd", 4, 0), ("wg", 3, 1), ("finish", 5), ("fwd", 5, 0),
+    ("trade", 4), ("sc", 2, 2), ("sc", 2, 3), ("sc", 3, 0), ("ggout", 0), ("wg", 4, 1),
+    ("total", 0), ("trade", 5), ("sc", 1, 3), ("total", 2), ("sc", 4, 0), ("wg", 4, 0),
+    ("sc", 5, 0), ("sc", 4, 1), ("wg", 5, 0), ("wg", 5, 1), ("sc", 3, 1), ("sc", 3, 2),
+    ("sc", 3, 3), ("total", 1), ("sc", 5, 1), ("sc", 5, 2), ("sc", 4, 2), ("sc", 4, 3),
+    ("ggin", 0), ("sc", 5, 3), ("total", 4), ("total", 5), ("total", 3),
 ]
 
 
@@ -129,14 +130,14 @@
     x_hbm, dy_hbm, gates_hbm, ids_hbm, table_hbm, wg_hbm, wu_hbm, wd_hbm,
     out_hbm, ggo_hbm, dwg_hbm, dwu_hbm, dwd_hbm,
     out_ref, ggo_ref, dwg_ref, dwu_ref, dwd_ref,
-    buf, gbuf, gcol, ggcol, ggs, ggr, w1, wd, dadb, hgb, acc1, acc2, dx, rc, rzu, rzd, ysend, ry, xsend, xr,
+    buf, gbuf, gcol, ggcol, ggs, ggr, w1, wd, dadb, hgb, acc1, acc2, dx, rc, rzu, rzd, ysend, ry, xsend, xr, dsend, dr,
     gates_ref, ids_ref, table_ref,
     local_sems, send_sems, recv_sems, pair_sems, gate_sem, gg_sem, twin_sems, chain_sems,
-    y_sems, x_sems, gate_sems,
+    y_sems, x_sems, gate_sems, spread_sems,
 ):
     f32, bf16 = jnp.float32, jnp.bfloat16
     devices = 4 * depth
-    early, wide = PAIR_FIRST, BOTH_COLUMNS
+    early, wide, straight = PAIR_FIRST, BOTH_COLUMNS, STRAIGHT
     counts = unit_counts(x_hbm.shape[0], devices)
     me, z, y, c, last = place(depth)
     tok, width = x_hbm.shape
@@ -176,7 +177,7 @@
     def rows_of(k):
         return pl.ds(*chunks[k])
 
-    OWN, PASS, WIDE, PAIR, CHAIN, THIN, TRADE, HOME, GATE, BACK, FLAT = range(11)
+    OWN, PASS, WIDE, PAIR, CHAIN, THIN, TRADE, HOME, GATE, BACK, FLAT, SPREAD = range(12)
 
     def push(group, cond, b, k, peer):
         block = lambda: buf.at[b(), :, rows_of(k)]
@@ -432,7 +433,41 @@
         out_ref[rows, :] = (mine + ry[rows, :].astype(f32)).astype(bf16)
         local(out_ref.at[rows], out_hbm.at[rows], 6).start()
 
+    def spread(k):
+        rows = rows_of(k)
+        turn = sum(straight[:k])
+        for i in range(depth):
+            zz = jnp.where(2 * z < depth, last - i, i)
+
+            def step():
+                dsend[zz, rows, :] = traded(k, zz).astype(bf16)
+
+            pl.when(zz != z)(step)
+            out.send(
+                SPREAD, zz != z,
+                remote(
+                    lambda: dsend.at[zz, rows, :], lambda: dr.at[z, rows, :],
+                    lambda: spread_sems.at[turn, z], lambda: index_of(zz, y, c),
+                ),
+            )
+
+    def collect(k):
+        rows = rows_of(k)
+        held = traded(k, z)
+        for i in range(1, depth):
+            src = (z + i) % depth
+            landed(dr.at[src, rows, :], spread_sems.at[sum(straight[:k]), src])
+            held = held + dr[src, rows, :].astype(f32)
+        out_ref[rows, :] = held.astype(bf16)
+        local(out_ref.at[rows], out_hbm.at[rows], 6).start()
+
     def scatter_point(k, p):
+        if straight[k]:
+            if p == 0:
+                spread(k)
+            elif p == depth - 1:
+                collect(k)
+            return
         if p == 0 and not early[k]:
             twin_sums(k)
         if p < depth - 1:
@@ -514,14 +549,17 @@
         pl.when(z == zz)(lambda: sent_blocks(zz))
     out.sent(PAIR, rc)
     late, soon = rows_in(early, False), rows_in(early, True)
+    direct = rows_in(straight, True)
     if late:
         out.sent(HOME, ysend.at[pl.ds(0, late)])
     if soon:
         out.sent(TRADE, xsend.at[:, pl.ds(0, soon)])
     if depth > 1 and late:
         out.sent(CHAIN, rzu.at[pl.ds(0, depth - 1), :, pl.ds(0, late)])
-    if depth > 1 and soon:
-        out.sent(THIN, rzu.at[pl.ds(0, depth - 1), 0, pl.ds(0, soon)])
+    if depth > 1 and soon > direct:
+        out.sent(THIN, rzu.at[pl.ds(0, depth - 1), 0, pl.ds(0, soon - direct)])
+    if depth > 1 and direct:
+        out.sent(SPREAD, dr.at[pl.ds(0, depth - 1), pl.ds(0, direct)])
     out.sent(BACK, ggs.at[pl.ds(0, devices - 1)])
     for copy in results:
         copy.wait()
@@ -558,12 +596,13 @@
             vmem((depth, 2, tok, width), bf16), vmem((depth, 2, tok, width), bf16),
             vmem((tok, width), bf16), vmem((tok, width), bf16),
             vmem((depth, tok, width), bf16), vmem((depth, tok, width), bf16),
+            vmem((depth, tok, width), bf16), vmem((depth, tok, width), bf16),
             vmem(gates.shape, bf16), vmem(ids.shape, ids.dtype),
             pltpu.SMEM(table.shape, table.dtype),
-            dma((12,)), dma((11,)), dma((n, devices // 2)), dma((n,)), dma, dma,
+            dma((12,)), dma((12,)), dma((n, devices // 2)), dma((n,)), dma, dma,
             dma((sum(unit_counts(tok, devices)),)), dma((n, depth + 1)),
             dma((max(1, n - sum(PAIR_FIRST)),)), dma((max(1, sum(PAIR_FIRST)), depth)),
-            dma((devices // 2,)),
+            dma((devices // 2,)), dma((max(1, sum(STRAIGHT)), depth)),
         ],
         compiler_params=pltpu.CompilerParams(
             collective_id=0, has_side_effects=True, vmem_limit_bytes=VMEM_GRANT

time: 74.2 us -> 72.6 us (0.978)
  Pallas kernels: 73.2 us -> 71.7 us
    pallas_call x1, Pallas kernels: 70.5 us -> 69 us  [fused_grads(): pl.pallas_call(lambda *refs: fused_kernel(depth, step_order(depth, n), ho...]
where the time goes in v4:
time: 72.6 us; the launch traced here: 72.5 us
  Pallas kernels  71.7 us (99%)
  between operations  0.8 us (1%)
    pallas_call x1, Pallas kernels, fused_grads(): pl.pallas_call(lambda *refs: fused_kernel(depth, step_order(depth, n), ho...  69 us
    pallas_call x1, Pallas kernels, store_all(): pl.pallas_call(lambda *refs: store_kernel(n, cuts, *refs), out_shape=[jax...  2.7 us

profile of v4, /device:TPU:0, one launch (start us, length us, event | category | flops | bytes accessed | tf_op | source)
XLA Modules:
  0.0 72.5 jit_solution(12801260656850495415)
XLA Ops:
  0.6 69.0 %shard_map.119 = (bf16[128,1024]{1,0:T(8,128)(2,1)}, bf16[8,128]{1,0:T(8,128)(2,1)}, bf16[1024,384]{1,0:T(8,128)(2,1)}, bf16[1024,384]{1,0:T(8,128)(2,1)}, bf16[384,1024]{1,0:T(8,128)(2,1)}) custom-call(bf16[128,1024]{1,0:T(8,128)(2,1)} %refs_0_.1, bf16[128,1024]{1,0:T(8,128)(2,1)} %refs_1_.1, bf16[8,128]{1,0:T(8,128)(2,1)} %bitcast.13, s32[8,128]{1,0:T(8,128)} %bitcast.12, ...), custom_call_target="tpu_custom_call" | custom-call | tf_op jit(solution)/shard_map/pallas_call | solution.py:578
  69.6 2.7 %shard_map.120 = (bf16[128,1024]{1,0:T(8,128)(2,1)}, bf16[8,128]{1,0:T(8,128)(2,1)}, bf16[1024,384]{1,0:T(8,128)(2,1)}, bf16[1024,384]{1,0:T(8,128)(2,1)}, bf16[384,1024]{1,0:T(8,128)(2,1)}) custom-call(bf16[128,1024]{1,0:T(8,128)(2,1)} %get-tuple-element.15.refs_0_, bf16[8,128]{1,0:T(8,128)(2,1)} %get-tuple-element.16.refs_1_, ...), custom_call_target="tpu_custom_call" | custom-call | tf_op jit(solution)/shard_map/pallas_call | solution.py:641

commit v5 on v4

--- a/solution.py
+++ b/solution.py
@@ -64,39 +64,43 @@
 
 
 TUNED_DEPTH = 4
-TUNED_SHARES = (16, 32, 32, 16, 16, 16)
-PAIR_FIRST = (False, False, True, True, True, True)
-STRAIGHT = (False, False, True, True, True, True)
-BOTH_COLUMNS = (False, False, False, True, True, False)
+TUNED_SHARES = (32, 16, 16, 16, 16, 16, 16)
+PAIR_FIRST = (False, True, True, True, True, True, True)
+STRAIGHT = (False, True, True, True, True, True, True)
+BOTH_COLUMNS = (False, True, False, False, False, False, True)
 TUNED = [
-    ("own", 0), ("gates", 0), ("own", 1), ("relay", 0, -1), ("relay", 0, 1), ("own", 3),
-    ("relay", 1, -1), ("relay", 0, -2), ("relay", 0, 2), ("cross", 0, 1), ("relay", 1, 1),
-    ("cross", 0, -1), ("relay", 0, 3), ("own", 2), ("relay", 0, -3), ("cross", 0, 0),
-    ("relay", 1, -2), ("relay", 1, 2), ("cross", 0, 2), ("cross", 0, -3), ("cross", 1, 0),
-    ("cross", 0, -2), ("cross", 0, 3), ("relay", 1, -3), ("relay", 1, 3), ("relay", 2, -1),
-    ("relay", 2, 1), ("cross", 1, 1), ("cross", 1, -1), ("finish", 0), ("fwd", 0, 0),
-    ("wg", 0, 0), ("relay", 2, -2), ("trade", 0), ("relay", 2, 2), ("cross", 3, 0),
-    ("cross", 2, 0), ("relay", 3, -1), ("wg", 0, 1), ("sc", 0, 0), ("cross", 1, -2),
-    ("cross", 1, 2), ("cross", 1, -3), ("relay", 2, -3), ("cross", 1, 3), ("relay", 2, 3),
-    ("own", 4), ("relay", 3, 1), ("own", 5), ("finish", 1), ("fwd", 1, 0), ("cross", 3, -1),
-    ("cross", 3, 1), ("fwd", 1, 1), ("cross", 2, -1), ("cross", 2, 1), ("wg", 1, 1),
-    ("relay", 5, -1), ("relay", 5, 1), ("relay", 3, 2), ("relay", 4, -1), ("sc", 0, 1),
-    ("cross", 2, 2), ("cross", 2, -2), ("trade", 1), ("cross", 2, -3), ("sc", 1, 0),
-    ("cross", 2, 3), ("wg", 1, 0), ("relay", 5, -2), ("cross", 3, -2), ("relay", 5, 2),
-    ("cross", 3, 2), ("cross", 4, 0), ("finish", 2), ("fwd", 2, 0), ("relay", 3, -2),
-    ("relay", 4, 1), ("fwd", 2, 1), ("relay", 5, 3), ("relay", 3, 3), ("relay", 5, -3),
-    ("sc", 0, 2), ("wg", 2, 1), ("cross", 3, 3), ("cross", 3, -3), ("wg", 2, 0), ("cross", 4, 1),
-    ("trade", 2), ("cross", 4, -1), ("cross", 5, 2), ("cross", 5, 1), ("relay", 3, -3),
-    ("relay", 4, 2), ("relay", 4, -2), ("sc", 1, 1), ("finish", 3), ("cross", 5, -1),
-    ("fwd", 3, 0), ("wg", 3, 0), ("cross", 5, 0), ("relay", 4, -3), ("cross", 5, 3),
-    ("cross", 4, -2), ("cross", 4, 2), ("sc", 0, 3), ("cross", 5, -2), ("cross", 5, -3),
-    ("sc", 2, 0), ("relay", 4, 3), ("cross", 4, 3), ("sc", 1, 2), ("sc", 2, 1), ("cross", 4, -3),
-    ("trade", 3), ("finish", 4), ("fwd", 4, 0), ("wg", 3, 1), ("finish", 5), ("fwd", 5, 0),
-    ("trade", 4), ("sc", 2, 2), ("sc", 2, 3), ("sc", 3, 0), ("ggout", 0), ("wg", 4, 1),
-    ("total", 0), ("trade", 5), ("sc", 1, 3), ("total", 2), ("sc", 4, 0), ("wg", 4, 0),
-    ("sc", 5, 0), ("sc", 4, 1), ("wg", 5, 0), ("wg", 5, 1), ("sc", 3, 1), ("sc", 3, 2),
-    ("sc", 3, 3), ("total", 1), ("sc", 5, 1), ("sc", 5, 2), ("sc", 4, 2), ("sc", 4, 3),
-    ("ggin", 0), ("sc", 5, 3), ("total", 4), ("total", 5), ("total", 3),
+    ("own", 0), ("gates", 0), ("own", 3), ("own", 1), ("relay", 0, 1), ("relay", 0, -1),
+    ("own", 2), ("cross", 1, 0), ("cross", 0, 1), ("relay", 0, -2), ("relay", 0, 2),
+    ("cross", 0, -1), ("relay", 2, 1), ("relay", 2, -1), ("cross", 1, -1), ("relay", 3, 1),
+    ("relay", 0, 3), ("relay", 0, -3), ("relay", 1, -1), ("relay", 3, -1), ("cross", 1, 1),
+    ("cross", 0, 0), ("relay", 1, 1), ("cross", 0, -2), ("own", 4), ("cross", 0, 2),
+    ("cross", 1, 2), ("cross", 0, 3), ("cross", 2, 1), ("relay", 3, 2), ("cross", 0, -3),
+    ("relay", 2, -2), ("cross", 2, -1), ("cross", 1, -2), ("relay", 1, -2), ("relay", 1, 2),
+    ("relay", 3, -2), ("cross", 3, 0), ("relay", 2, 2), ("own", 5), ("finish", 0), ("fwd", 0, 0),
+    ("fwd", 0, 1), ("relay", 4, 1), ("relay", 2, -3), ("cross", 1, 3), ("own", 6),
+    ("cross", 2, -2), ("trade", 0), ("wg", 0, 0), ("relay", 1, 3), ("relay", 1, -3), ("sc", 0, 0),
+    ("cross", 2, 2), ("cross", 3, -2), ("cross", 1, -3), ("cross", 4, 0), ("relay", 3, -3),
+    ("relay", 3, 3), ("relay", 4, -1), ("relay", 2, 3), ("cross", 2, -3), ("cross", 2, 0),
+    ("finish", 1), ("fwd", 1, 0), ("cross", 3, 2), ("relay", 5, -1), ("relay", 5, 1),
+    ("cross", 5, 0), ("relay", 4, 2), ("wg", 0, 1), ("cross", 3, -1), ("wg", 1, 1),
+    ("cross", 6, 0), ("cross", 2, 3), ("cross", 3, 1), ("relay", 4, -2), ("wg", 1, 0),
+    ("relay", 6, -1), ("trade", 1), ("cross", 3, -3), ("sc", 0, 1), ("cross", 3, 3),
+    ("finish", 2), ("fwd", 2, 0), ("cross", 5, -1), ("relay", 4, 3), ("relay", 5, 2),
+    ("wg", 2, 0), ("relay", 6, 1), ("cross", 4, 1), ("relay", 4, -3), ("cross", 6, 1),
+    ("relay", 5, -2), ("finish", 3), ("fwd", 3, 0), ("relay", 5, 3), ("cross", 6, -1),
+    ("wg", 2, 1), ("wg", 3, 1), ("cross", 4, 2), ("relay", 5, -3), ("trade", 2), ("cross", 4, -3),
+    ("relay", 6, 2), ("cross", 4, -1), ("cross", 4, 3), ("relay", 6, -2), ("cross", 4, -2),
+    ("sc", 1, 0), ("cross", 5, 1), ("trade", 3), ("wg", 3, 0), ("sc", 1, 1), ("cross", 5, -2),
+    ("cross", 6, 2), ("cross", 6, -2), ("cross", 5, 2), ("sc", 0, 2), ("relay", 6, -3),
+    ("finish", 4), ("cross", 5, 3), ("cross", 5, -3), ("fwd", 4, 0), ("finish", 5), ("fwd", 5, 0),
+    ("cross", 6, -3), ("wg", 4, 1), ("relay", 6, 3), ("sc", 1, 2), ("sc", 1, 3), ("sc", 2, 0),
+    ("trade", 4), ("cross", 6, 3), ("sc", 2, 1), ("wg", 4, 0), ("sc", 3, 0), ("trade", 5),
+    ("sc", 3, 1), ("sc", 2, 2), ("finish", 6), ("fwd", 6, 0), ("ggout", 0), ("sc", 4, 0),
+    ("wg", 5, 0), ("trade", 6), ("sc", 5, 0), ("sc", 0, 3), ("sc", 4, 1), ("sc", 6, 0),
+    ("wg", 6, 0), ("sc", 5, 1), ("wg", 5, 1), ("ggin", 0), ("total", 1), ("sc", 3, 2),
+    ("sc", 3, 3), ("sc", 4, 2), ("sc", 5, 2), ("total", 3), ("sc", 2, 3), ("total", 0),
+    ("sc", 6, 1), ("sc", 4, 3), ("sc", 6, 2), ("sc", 5, 3), ("wg", 6, 1), ("sc", 6, 3),
+    ("total", 5), ("total", 6), ("total", 2), ("total", 4),
 ]
 
 
@@ -392,7 +396,7 @@
             piece = ref.at[zz, 0, rows, :] if early[k] else ref.at[zz, :, rows, :]
 
             def step():
-                pl.when(has)(lambda: landed(piece, chain_sems.at[k, zz + way]))
+                pl.when(has)(lambda: landed(piece, chain_sems.at[k - sum(straight[:k]), zz + way]))
                 if early[k]:
                     held = ref[zz, 0, rows, :].astype(f32)
                     ref[zz, 0, rows, :] = (traded(k, zz) + held).astype(bf16)
@@ -403,14 +407,14 @@
             pl.when(there)(step)
             out.send(
                 THIN if early[k] else CHAIN, there,
-                remote(lambda: piece, lambda: piece, lambda: chain_sems.at[k, zz + way], peer),
+                remote(lambda: piece, lambda: piece, lambda: chain_sems.at[k - sum(straight[:k]), zz + way], peer),
             )
 
     def home(k):
         rows = rows_of(k)
         way = 0 if early[k] else slice(None)
-        pl.when(z > 0)(lambda: landed(rzu.at[z, way, rows, :], chain_sems.at[k, z + 1]))
-        pl.when(z < last)(lambda: landed(rzd.at[z, way, rows, :], chain_sems.at[k, z]))
+        pl.when(z > 0)(lambda: landed(rzu.at[z, way, rows, :], chain_sems.at[k - sum(straight[:k]), z + 1]))
+        pl.when(z < last)(lambda: landed(rzd.at[z, way, rows, :], chain_sems.at[k - sum(straight[:k]), z]))
         if early[k]:
             held = rzu[z, 0, rows, :].astype(f32) + rzd[z, 0, rows, :].astype(f32)
             out_ref[rows, :] = (traded(k, z) + held).astype(bf16)
@@ -600,7 +604,7 @@
             vmem(gates.shape, bf16), vmem(ids.shape, ids.dtype),
             pltpu.SMEM(table.shape, table.dtype),
             dma((12,)), dma((12,)), dma((n, devices // 2)), dma((n,)), dma, dma,
-            dma((sum(unit_counts(tok, devices)),)), dma((n, depth + 1)),
+            dma((sum(unit_counts(tok, devices)),)), dma((max(1, n - sum(STRAIGHT)), depth + 1)),
             dma((max(1, n - sum(PAIR_FIRST)),)), dma((max(1, sum(PAIR_FIRST)), depth)),
             dma((devices // 2,)), dma((max(1, sum(STRAIGHT)), depth)),
         ],

time: 72.6 us -> 72.3 us (level)
  no operation moved by 1% of the time
where the time goes in v5:
time: 72.3 us; the launch traced here: 72.1 us
  Pallas kernels  71.3 us (99%)
  between operations  0.8 us (1%)
    pallas_call x1, Pallas kernels, fused_grads(): pl.pallas_call(lambda *refs: fused_kernel(depth, step_order(depth, n), ho...  68.6 us
    pallas_call x1, Pallas kernels, store_all(): pl.pallas_call(lambda *refs: store_kernel(n, cuts, *refs), out_shape=[jax...  2.7 us

profile of v5, /device:TPU:0, one launch (start us, length us, event | category | flops | bytes accessed | tf_op | source)
XLA Modules:
  0.0 72.1 jit_solution(14632813600571184548)
XLA Ops:
  0.6 68.6 %shard_map.119 = (bf16[128,1024]{1,0:T(8,128)(2,1)}, bf16[8,128]{1,0:T(8,128)(2,1)}, bf16[1024,384]{1,0:T(8,128)(2,1)}, bf16[1024,384]{1,0:T(8,128)(2,1)}, bf16[384,1024]{1,0:T(8,128)(2,1)}) custom-call(bf16[128,1024]{1,0:T(8,128)(2,1)} %refs_0_.1, bf16[128,1024]{1,0:T(8,128)(2,1)} %refs_1_.1, bf16[8,128]{1,0:T(8,128)(2,1)} %bitcast.13, s32[8,128]{1,0:T(8,128)} %bitcast.12, ...), custom_call_target="tpu_custom_call" | custom-call | tf_op jit(solution)/shard_map/pallas_call | solution.py:582
  69.2 2.7 %shard_map.120 = (bf16[128,1024]{1,0:T(8,128)(2,1)}, bf16[8,128]{1,0:T(8,128)(2,1)}, bf16[1024,384]{1,0:T(8,128)(2,1)}, bf16[1024,384]{1,0:T(8,128)(2,1)}, bf16[384,1024]{1,0:T(8,128)(2,1)}) custom-call(bf16[128,1024]{1,0:T(8,128)(2,1)} %get-tuple-element.15.refs_0_, bf16[8,128]{1,0:T(8,128)(2,1)} %get-tuple-element.16.refs_1_, ...), custom_call_target="tpu_custom_call" | custom-call | tf_op jit(solution)/shard_map/pallas_call | solution.py:645

commit v6 on v5

--- a/solution.py
+++ b/solution.py
@@ -317,13 +317,25 @@
         for j in range(nb):
             held = jnp.where(spot == p0 * 4 + j, gate_grad[j * size : (j + 1) * size], held)
         ggcol[rows, :] = held
-        src = lambda: dx.at[pl.ds(p0, planes), :, 1 - c, rows, :]
-        dst = lambda: rc.at[pl.ds(p0, planes), :, rows, :]
-        out.send(PAIR, None, remote(src, dst, lambda: twin_sems.at[sum(counts[:k]) + u], twin))
+        for j, (q0, span) in enumerate(twin_parts(k)):
+            if counts[k] == 1 or j == u:
+                src = lambda: dx.at[pl.ds(q0, span), :, 1 - c, rows, :]
+                dst = lambda: rc.at[pl.ds(q0, span), :, rows, :]
+                out.send(PAIR, None, remote(src, dst, lambda: twin_sems.at[k, j], twin))
+
+    def twin_parts(k):
+        if depth % 2:
+            return [(0, depth)]
+        first = jnp.where(z < half, half, 0)
+        return [(first, half), (half - first, half)]
+
+    def twin_sum(k, j):
+        q0, span = twin_parts(k)[j]
+        landed(rc.at[pl.ds(q0, span), :, rows_of(k), :], twin_sems.at[k, j])
 
     def twin_sums(k):
-        for u, (p0, planes) in enumerate(units(k)):
-            landed(rc.at[pl.ds(p0, planes), :, rows_of(k), :], twin_sems.at[sum(counts[:k]) + u])
+        for j in range(len(twin_parts(k))):
+            twin_sum(k, j)
 
     tile = 256 if width % 256 == 0 else 128
 
@@ -370,9 +382,11 @@
     def trade(k):
         if not early[k]:
             return
-        twin_sums(k)
         rows = rows_of(k)
+        parts = len(twin_parts(k))
         for i in range(depth):
+            if i * parts % depth == 0:
+                twin_sum(k, i * parts // depth)
             zz = jnp.where(2 * z < depth, last - i, i)
             xsend[zz, rows, :] = part_sum(zz, 1 - y, rows, ()).astype(bf16)
             out.send(
@@ -604,7 +618,7 @@
             vmem(gates.shape, bf16), vmem(ids.shape, ids.dtype),
             pltpu.SMEM(table.shape, table.dtype),
             dma((12,)), dma((12,)), dma((n, devices // 2)), dma((n,)), dma, dma,
-            dma((sum(unit_counts(tok, devices)),)), dma((max(1, n - sum(STRAIGHT)), depth + 1)),
+            dma((n, 2)), dma((max(1, n - sum(STRAIGHT)), depth + 1)),
             dma((max(1, n - sum(PAIR_FIRST)),)), dma((max(1, sum(PAIR_FIRST)), depth)),
             dma((devices // 2,)), dma((max(1, sum(STRAIGHT)), depth)),
         ],

time: 72.3 us -> 72.3 us (level)
  no operation moved by 1% of the time
where the time goes in v6:
time: 72.3 us; the launch traced here: 72.1 us
  Pallas kernels  71.3 us (99%)
  between operations  0.8 us (1%)
    pallas_call x1, Pallas kernels, fused_grads(): pl.pallas_call(lambda *refs: fused_kernel(depth, step_order(depth, n), ho...  68.6 us
    pallas_call x1, Pallas kernels, store_all(): pl.pallas_call(lambda *refs: store_kernel(n, cuts, *refs), out_shape=[jax...  2.7 us

profile of v6, /device:TPU:0, one launch (start us, length us, event | category | flops | bytes accessed | tf_op | source)
XLA Modules:
  0.0 72.1 jit_solution(14092347015007560057)
XLA Ops:
  0.6 68.6 %shard_map.119 = (bf16[128,1024]{1,0:T(8,128)(2,1)}, bf16[8,128]{1,0:T(8,128)(2,1)}, bf16[1024,384]{1,0:T(8,128)(2,1)}, bf16[1024,384]{1,0:T(8,128)(2,1)}, bf16[384,1024]{1,0:T(8,128)(2,1)}) custom-call(bf16[128,1024]{1,0:T(8,128)(2,1)} %refs_0_.1, bf16[128,1024]{1,0:T(8,128)(2,1)} %refs_1_.1, bf16[8,128]{1,0:T(8,128)(2,1)} %bitcast.13, s32[8,128]{1,0:T(8,128)} %bitcast.12, ...), custom_call_target="tpu_custom_call" | custom-call | tf_op jit(solution)/shard_map/pallas_call | solution.py:596
  69.3 2.7 %shard_map.120 = (bf16[128,1024]{1,0:T(8,128)(2,1)}, bf16[8,128]{1,0:T(8,128)(2,1)}, bf16[1024,384]{1,0:T(8,128)(2,1)}, bf16[1024,384]{1,0:T(8,128)(2,1)}, bf16[384,1024]{1,0:T(8,128)(2,1)}) custom-call(bf16[128,1024]{1,0:T(8,128)(2,1)} %get-tuple-element.15.refs_0_, bf16[8,128]{1,0:T(8,128)(2,1)} %get-tuple-element.16.refs_1_, ...), custom_call_target="tpu_custom_call" | custom-call | tf_op jit(solution)/shard_map/pallas_call | solution.py:659
